TPU v7x, 256 devices: a whole 4x4x8 slice. The times are simulated.
256 devices in a mesh: seq: 16 (over x, y), exp: 16 (over z, core).
Axes of the slice: x: 4, y: 4, z: 8, core: 2. Of those that a mesh axis runs over, the one named last changes fastest.
Arguments:
- tokens: bfloat16 [32, 1024, 1152], P('exp', 'seq'), may hold values from -80 to 80
- timesteps: int32 [32], P('exp'), may hold values from 0 to 63
- modulation: bfloat16 [64, 2, 1152], replicated, may hold values from -0.5 to 0.5
- routes: int32 [16, 1024, 2, 2], P('exp', 'seq'), may hold values from 0 to 15, all different within a row; in each aligned block of 128 rows (0 to 127, 128 to 255, ..., all dimensions but the last counted through in order) at most 17 rows name the same one
- gate_codes: int32 [32, 1024, 2], P('exp', 'seq'), may hold values from 1 to 16
- gate_weight: bfloat16 [16, 1152, 4608], P('exp', None, 'seq'), may hold values from -0.1875 to 0.1875
- up_weight: bfloat16 [16, 1152, 4608], P('exp', None, 'seq'), may hold values from -0.1875 to 0.1875
- down_weight: bfloat16 [16, 4608, 1152], P('exp', 'seq'), may hold values from -0.09375 to 0.09375
- cotangent: bfloat16 [32, 1024, 1152], P('exp', 'seq'), may hold values from -6 to 6
Outputs:
- grad_tokens: bfloat16 [32, 1024, 1152], P('exp', 'seq')
Inputs may be any that keep to these rules, and one draw needn't show every extreme that they name: `routes`: among the rows of one device (entries [g, p, i, :] with p in one block of 64 patches, all i) no expert is named more than 17 times, a bound that some block reaches.
All inputs are finite; a program needn't handle non-finite values.
Results may differ from a plain program's by a relative error of at most 0.015.
Values may be sent and summed in bfloat16 or wider, within the bound.
A program may use at most 192 MiB of HBM per device.

v0:
```python
import jax
import jax.numpy as jnp
from jax import lax
from jax.sharding import PartitionSpec as P


def in_one_piece(arrays, axis, split_dim, concat_dim, along):
    ends, at = ([], 0)
    for a in arrays[:-1]:
        at += a.shape[along]
        ends.append(at)
    both = jnp.concatenate(arrays, axis=along)
    return tuple(
        jnp.split(
            lax.all_to_all(both, axis, split_axis=split_dim, concat_axis=concat_dim, tiled=True),
            ends,
            axis=along,
        )
    )


def normalize_modulate(tokens_f, shift, scale):
    mean_square = jnp.mean(tokens_f * tokens_f, axis=-1, keepdims=True)
    return tokens_f / jnp.sqrt(mean_square + 1e-06) * (1.0 + scale) + shift


def per_device(
    tokens,
    timesteps,
    modulation,
    routes,
    gate_codes,
    gate_weight,
    up_weight,
    down_weight,
    cotangent,
):
    img_local, patch_local, feature_width = tokens.shape
    top_count = routes.shape[3]
    row_count = img_local * patch_local
    n_exp = lax.axis_size("exp")
    local_experts = gate_weight.shape[0]
    block_width = gate_weight.shape[2]
    expert_count = local_experts * n_exp
    capacity = top_count * row_count // expert_count + 1
    slot_count = expert_count * capacity
    level_count = modulation.shape[0]
    select = (timesteps[:, None] == jnp.arange(level_count, dtype=jnp.int32)[None, :]).astype(
        jnp.float32
    )
    table = jnp.dot(
        select,
        modulation.astype(jnp.float32).reshape(level_count, 2 * feature_width),
        precision=lax.Precision.HIGHEST,
    )
    table = jnp.broadcast_to(
        table[:, None, :], (img_local, patch_local, 2 * feature_width)
    ).reshape(row_count, 2 * feature_width)
    scale = table[:, :feature_width]
    shift = table[:, feature_width:]
    tokens_f = tokens.reshape(row_count, feature_width).astype(jnp.float32)
    pre, pullback = jax.vjp(lambda value: normalize_modulate(value, shift, scale), tokens_f)
    normed = pre.astype(jnp.bfloat16)
    codes = gate_codes.reshape(row_count, top_count).astype(jnp.float32)
    route_weight = codes / jnp.sum(codes, axis=-1, keepdims=True)
    flat_routes = jnp.transpose(routes[0], (1, 0, 2)).reshape(row_count * top_count)
    expert_hot = (
        flat_routes[:, None] == jnp.arange(expert_count, dtype=jnp.int32)[None, :]
    ).astype(jnp.int32)
    earlier = jnp.cumsum(expert_hot, axis=0) - expert_hot
    position = jnp.sum(earlier * expert_hot, axis=1)
    slot_ids = flat_routes * capacity + position
    slot_hot = (slot_ids[:, None] == jnp.arange(slot_count, dtype=jnp.int32)[None, :]).astype(
        jnp.float32
    )
    slot_hot = slot_hot.reshape(row_count, top_count, slot_count)
    member = jnp.sum(slot_hot, axis=1)
    weighted = jnp.sum(slot_hot * route_weight[:, :, None], axis=1)
    contract_tokens = (((0,), (0,)), ((), ()))
    send_rows = lax.dot_general(
        member.astype(jnp.bfloat16), normed, contract_tokens, preferred_element_type=jnp.float32
    ).astype(jnp.bfloat16)
    grads_f = cotangent.reshape(row_count, feature_width).astype(jnp.float32)
    send_grads = lax.dot_general(
        weighted, grads_f, contract_tokens, precision=lax.Precision.HIGHEST
    ).astype(jnp.bfloat16)
    send_rows = send_rows.reshape(n_exp, local_experts * capacity, feature_width)
    send_grads = send_grads.reshape(n_exp, local_experts * capacity, feature_width)
    arrived_rows, arrived_grads = in_one_piece((send_rows, send_grads), "exp", 0, 0, 1)

    def by_expert(arrived):
        shaped = arrived.reshape(n_exp, local_experts, capacity, feature_width)
        return jnp.transpose(shaped, (1, 0, 2, 3)).reshape(
            local_experts, n_exp * capacity, feature_width
        )

    rows_all = by_expert(arrived_rows)
    grads_all = by_expert(arrived_grads)
    weight_stack = jnp.stack([gate_weight, up_weight, jnp.swapaxes(down_weight, 1, 2)], axis=1)
    piece = lax.all_gather(weight_stack, "seq", axis=3, tiled=True)
    count = piece.shape[3] // block_width
    shaped = piece.reshape(local_experts, 3, feature_width, count, block_width)
    gate_part = shaped[0, 0]
    up_part = shaped[0, 1]
    down_part = shaped[0, 2]
    rows_in = rows_all[0]
    grads_in = grads_all[0]
    gate_pre = jnp.einsum("rd,dkf->krf", rows_in, gate_part, preferred_element_type=jnp.float32)
    up_pre = jnp.einsum("rd,dkf->krf", rows_in, up_part, preferred_element_type=jnp.float32)
    grad_hidden = jnp.einsum("rd,dkf->krf", grads_in, down_part, preferred_element_type=jnp.float32)
    sigma = jax.nn.sigmoid(gate_pre)
    silu_gate = gate_pre * sigma
    grad_gate_pre = (grad_hidden * up_pre * sigma * (1.0 + gate_pre * (1.0 - sigma))).astype(
        jnp.bfloat16
    )
    grad_up_pre = (grad_hidden * silu_gate).astype(jnp.bfloat16)
    back_term = jnp.einsum(
        "krf,dkf->krd", grad_gate_pre, gate_part, preferred_element_type=jnp.float32
    )
    back_term = back_term + jnp.einsum(
        "krf,dkf->krd", grad_up_pre, up_part, preferred_element_type=jnp.float32
    )
    back_term = back_term.astype(jnp.bfloat16).astype(jnp.float32)
    results = [jnp.sum(back_term, axis=0)]
    folded = jnp.stack(results)
    folded = folded.reshape(local_experts, n_exp, capacity, feature_width)
    slot_source = jnp.transpose(folded, (1, 0, 2, 3)).reshape(
        n_exp, local_experts * capacity, feature_width
    )
    slot_source = slot_source.astype(jnp.bfloat16)
    slot_backs = lax.all_to_all(slot_source, "exp", split_axis=0, concat_axis=0, tiled=True)
    slot_backs = slot_backs.reshape(slot_count, feature_width).astype(jnp.float32)
    grad_normed = jnp.dot(member, slot_backs, precision=lax.Precision.HIGHEST)
    grad_tokens = pullback(grad_normed)[0]
    return grad_tokens.astype(jnp.bfloat16).reshape(img_local, patch_local, feature_width)


def solution(mesh):
    in_specs = (
        P("exp", "seq", None),
        P("exp"),
        P(),
        P("exp", "seq", None, None),
        P("exp", "seq", None),
        P("exp", None, "seq"),
        P("exp", None, "seq"),
        P("exp", "seq", None),
        P("exp", "seq", None),
    )
    out_specs = P("exp", "seq", None)
    return jax.shard_map(
        per_device, mesh=mesh, in_specs=in_specs, out_specs=out_specs, check_vma=False
    )
```

profile of v0, /device:TPU:1, one launch (start us, length us, event | category | flops | bytes accessed | tf_op | source)
XLA Modules:
  0.0 319.6 jit_solution(1848872654035132093)
XLA Ops:
  6.6 3.1 pad_maximum_fusion
  9.7 0.8 copy.19
  10.8 0.7 convert_element_type.73
  11.5 0.7 convert_reduce_fusion.1
  12.2 1.1 fusion.22
  13.4 0.7 broadcast_multiply_fusion
  14.3 0.6 reduce-window.6
  15.6 0.7 convolution_convert_fusion
  17.0 1.2 convolution_convert_fusion.1
  18.1 1.3 reshape.136
  19.4 0.3 pad_maximum_fusion.1
  19.7 47.3 %all_to_all.10 = bf16[16,34,1152]{2,1,0:T(8,128)(2,1)S(1)} all-to-all(bf16[16,34,1152]{2,1,0:T(8,128)(2,1)S(1)} %pad_maximum_fusion.1), channel_id=1, replica_groups=mesh['seq'=16,'exp'=16] {'exp'}, dimensions={0} | all-to-all | bytes 2506752 | tf_op jit(solution)/shard_map/all_to_all | solution.py:15
  67.1 0.2 fusion.37
  67.3 1.1 reshape.142
  68.6 138.1 %all-gather.2.cloned.1.call-done = bf16[1,3,1152,4608]{2,3,1,0:T(8,128)(2,1)} async-done(((bf16[1,3,1152,288]{2,3,1,0:T(8,128)(2,1)}), bf16[1,3,1152,4608]{2,3,1,0:T(8,128)(2,1)}) %all-gather.2.cloned.1.call-update) | async-done | bytes 31850512 | tf_op jit(solution)/shard_map/all_gather | solution.py:100
  206.7 14.3 %fusion = f32[16,288,272]{1,2,0:T(8,128)} fusion(bf16[272,1152,1]{1,0,2:T(8,128)(2,1)} %reshape.142, bf16[1,3,1152,16,288]{2,4,3,1,0:T(8,128)(2,1)} %bitcast.127), kind=kOutput, calls=%fused_computation.4 | convolution fusion | flops 2887778304 | bytes 16257024 | tf_op jit(solution)/shard_map/rd,dkf->krf/dot_general | solution.py:110
  221.0 14.3 %fusion.3 = f32[16,288,272]{1,2,0:T(8,128)} fusion(bf16[272,1152,1]{1,0,2:T(8,128)(2,1)S(1)} %reshape.143, bf16[1,3,1152,16,288]{2,4,3,1,0:T(8,128)(2,1)} %bitcast.128), kind=kOutput, calls=%fused_computation.7 | convolution fusion | flops 2887778304 | bytes 16257024 | tf_op jit(solution)/shard_map/rd,dkf->krf/dot_general | solution.py:108
  235.3 24.0 %fusion.2 = f32[16,272,1152]{2,1,0:T(8,128)} fusion(bf16[1,3,1152,16,288]{2,4,3,1,0:T(8,128)(2,1)} %bitcast.129, f32[16,288,272]{1,2,0:T(8,128)} %fusion.3, f32[16,288,272]{1,2,0:T(8,128)} %fusion, bf16[272,1152,1]{1,0,2:T(8,128)(2,1)S(1)} %reshape.143), kind=kOutput, calls=%fused_computation.6 | convolution fusion | flops 5788090368 | bytes 55283712 | tf_op jit(solution)/shard_map/krf,dkf->krd/dot_general | solution.py:117
  259.3 17.7 %fusion.17 = bf16[272,1152]{1,0:T(8,128)(2,1)S(1)} fusion(f32[16,272,1152]{2,1,0:T(8,128)} %fusion.2, bf16[1,3,1152,16,288]{2,4,3,1,0:T(8,128)(2,1)} %bitcast.130, f32[16,288,272]{1,2,0:T(8,128)} %fusion.3, f32[16,288,272]{1,2,0:T(8,128)} %fusion), kind=kOutput, calls=%fused_computation.27 | convolution fusion | flops 2910025728 | bytes 44666880 | tf_op jit(solution)/shard_map/krf,dkf->krd/dot_general | solution.py:120
  277.0 1.1 convert_element_type.79
  278.1 7.9 %all-to-all-start.1 = ((bf16[16,17,1152]{2,1,0:T(8,128)(2,1)}), bf16[16,17,1152]{2,1,0:T(8,128)(2,1)S(1)}, u32[]{:S(2)}, u32[]{:S(2)}) async-start(bf16[16,17,1152]{2,1,0:T(8,128)(2,1)} %convert_element_type.79), calls=%async_computation.1 | async-start | bytes 1769472 | tf_op jit(solution)/shard_map/all_to_all | solution.py:131
  286.1 24.6 %all-to-all-done.1 = bf16[16,17,1152]{2,1,0:T(8,128)(2,1)S(1)} async-done(((bf16[16,17,1152]{2,1,0:T(8,128)(2,1)}), bf16[16,17,1152]{2,1,0:T(8,128)(2,1)S(1)}, u32[]{:S(2)}, u32[]{:S(2)}) %all-to-all-start.1) | async-done | bytes 626720 | tf_op jit(solution)/shard_map/all_to_all | solution.py:131
  310.9 0.9 fusion.24
  311.8 0.9 fusion.20
  (45 shorter events, 2.6 us)
Async XLA Ops:
  6.5 9.0 %copy-start = (bf16[2,64,1152]{2,1,0:T(8,128)(2,1)S(1)}, bf16[2,64,1152]{2,1,0:T(8,128)(2,1)}, u32[]{:S(2)}) copy-start(bf16[2,64,1152]{2,1,0:T(8,128)(2,1)} %param.17) | copy-start | bytes 884740
  6.5 10.2 %copy-start.2 = (bf16[2,64,1152]{2,1,0:T(8,128)(2,1)S(1)}, bf16[2,64,1152]{2,1,0:T(8,128)(2,1)}, u32[]{:S(2)}) copy-start(bf16[2,64,1152]{2,1,0:T(8,128)(2,1)} %param.9) | copy-start | bytes 884740
  6.5 8.9 %copy-start.5 = (bf16[64,2,1152]{2,1,0:T(2,128)(2,1)S(1)}, bf16[64,2,1152]{2,1,0:T(2,128)(2,1)}, u32[]{:S(2)}) copy-start(bf16[64,2,1152]{2,1,0:T(2,128)(2,1)} %param.11) | copy-start | bytes 884740
  6.5 9.9 %copy-start.6 = (s32[2]{0:T(128)S(1)}, s32[2]{0:T(128)}, u32[]{:S(2)}) copy-start(s32[2]{0:T(128)} %param.10) | copy-start | bytes 28
  6.5 200.2 %all-gather.2.cloned.1.call-start = ((), (), s32[]{:S(2)}) async-start(), calls=%async_computation.2 | async-start | bytes 33841152 | tf_op jit(solution)/shard_map/all_gather | solution.py:100
  15.6 1.4 copy-start.3
  259.3 51.6 %copy-start.4 = (f32[128,272]{0,1:T(8,128)S(1)}, f32[128,272]{0,1:T(8,128)}, u32[]{:S(2)}) copy-start(f32[128,272]{0,1:T(8,128)} %copy-done.3) | copy-start | bytes 417796
  259.3 53.4 %copy-start.1 = (bf16[2,64,1152]{2,1,0:T(8,128)(2,1)S(1)}, bf16[2,64,1152]{2,1,0:T(8,128)(2,1)}, u32[]{:S(2)}) copy-start(bf16[2,64,1152]{2,1,0:T(8,128)(2,1)} %param.17) | copy-start | bytes 884740
  278.1 32.6 %all-to-all-start.1 = ((bf16[16,17,1152]{2,1,0:T(8,128)(2,1)}), bf16[16,17,1152]{2,1,0:T(8,128)(2,1)S(1)}, u32[]{:S(2)}, u32[]{:S(2)}) async-start(bf16[16,17,1152]{2,1,0:T(8,128)(2,1)} %convert_element_type.79), calls=%async_computation.1 | async-start | bytes 1769472 | tf_op jit(solution)/shard_map/all_to_all | solution.py:131
Sparse Core Ops, SparseCore 0:
  9.8 196.8 all-gather.1
where the time goes:
time: 320 us
  waiting for transfers between devices  163 us (51%)
  matrix products  73.1 us (23%)
  blocking collectives  47.3 us (15%)
  between operations  13.6 us (4%)
  other arithmetic  8.44 us (3%)
  starting transfers between devices  7.89 us (2%)
  local copies, waits for them, and re-layouts  6.47 us (2%)
    all_gather x1, waiting for transfers between devices, per_device(): piece = lax.all_gather(weight_stack, 'seq', axis=3, tiled=True)  138 us
    all_to_all x1, blocking collectives, in_one_piece(): lax.all_to_all(both, axis, split_axis=split_dim, concat_axis=concat_dim,...  47.3 us
    all_to_all x1, waiting for transfers between devices, per_device(): lax.all_to_all(slot_source, 'exp', split_axis=0, concat_axis=0, tiled=True)  24.6 us
    dot_general x1, matrix products, per_device(): jnp.einsum('krf,dkf->krd', grad_gate_pre, gate_part, preferred_element_ty...  24 us
    dot_general x1, matrix products, per_device(): jnp.einsum('krf,dkf->krd', grad_up_pre, up_part, preferred_element_type=j...  17.7 us
    dot_general x1, matrix products, per_device(): jnp.einsum('rd,dkf->krf', grads_in, down_part, preferred_element_type=jnp...  14.3 us
    dot_general x1, matrix products, per_device(): jnp.einsum('rd,dkf->krf', rows_in, gate_part, preferred_element_type=jnp....  14.3 us
    all_to_all x1, starting transfers between devices, per_device(): lax.all_to_all(slot_source, 'exp', split_axis=0, concat_axis=0, tiled=True)  7.86 us
  transfers between devices with their start and end apart: 2, of which 2 were waited for; matrix products, arithmetic and copies ran while one was open for 4% of the time, Pallas kernels for 0%

commit v1 on v0

v1 whole, which is shorter than its diff:
```python
import jax
import jax.numpy as jnp
from jax import lax
from jax.sharding import PartitionSpec as P


def normalize_modulate(tokens_f, shift, scale):
    mean_square = jnp.mean(tokens_f * tokens_f, axis=-1, keepdims=True)
    return tokens_f / jnp.sqrt(mean_square + 1e-06) * (1.0 + scale) + shift


def per_device(
    tokens,
    timesteps,
    modulation,
    routes,
    gate_codes,
    gate_weight,
    up_weight,
    down_weight,
    cotangent,
):
    img_local, patch_local, feature_width = tokens.shape
    top_count = routes.shape[3]
    row_count = img_local * patch_local
    n_exp = lax.axis_size("exp")
    local_experts = gate_weight.shape[0]
    block_width = gate_weight.shape[2]
    expert_count = local_experts * n_exp
    capacity = top_count * row_count // expert_count + 1
    slot_count = expert_count * capacity
    level_count = modulation.shape[0]
    select = (timesteps[:, None] == jnp.arange(level_count, dtype=jnp.int32)[None, :]).astype(
        jnp.float32
    )
    table = jnp.dot(
        select,
        modulation.astype(jnp.float32).reshape(level_count, 2 * feature_width),
        precision=lax.Precision.HIGHEST,
    )
    table = jnp.broadcast_to(
        table[:, None, :], (img_local, patch_local, 2 * feature_width)
    ).reshape(row_count, 2 * feature_width)
    scale = table[:, :feature_width]
    shift = table[:, feature_width:]
    tokens_f = tokens.reshape(row_count, feature_width).astype(jnp.float32)
    pre, pullback = jax.vjp(lambda value: normalize_modulate(value, shift, scale), tokens_f)
    normed = pre.astype(jnp.bfloat16)
    codes = gate_codes.reshape(row_count, top_count).astype(jnp.float32)
    route_weight = codes / jnp.sum(codes, axis=-1, keepdims=True)
    flat_routes = jnp.transpose(routes[0], (1, 0, 2)).reshape(row_count * top_count)
    expert_hot = (
        flat_routes[:, None] == jnp.arange(expert_count, dtype=jnp.int32)[None, :]
    ).astype(jnp.int32)
    earlier = jnp.cumsum(expert_hot, axis=0) - expert_hot
    position = jnp.sum(earlier * expert_hot, axis=1)
    slot_ids = flat_routes * capacity + position
    slot_hot = (slot_ids[:, None] == jnp.arange(slot_count, dtype=jnp.int32)[None, :]).astype(
        jnp.float32
    )
    slot_hot = slot_hot.reshape(row_count, top_count, slot_count)
    member = jnp.sum(slot_hot, axis=1)
    weighted = jnp.sum(slot_hot * route_weight[:, :, None], axis=1)
    contract_tokens = (((0,), (0,)), ((), ()))
    member16 = member.astype(jnp.bfloat16)
    send_rows = lax.dot_general(
        member16, normed, contract_tokens, preferred_element_type=jnp.float32
    ).astype(jnp.bfloat16)
    slot_weight = jnp.sum(weighted, axis=0)
    picked = lax.dot_general(
        member16,
        cotangent.reshape(row_count, feature_width),
        contract_tokens,
        preferred_element_type=jnp.float32,
    )
    send_grads = (picked * slot_weight[:, None]).astype(jnp.bfloat16)
    weight_stack = jnp.stack(
        [jnp.swapaxes(gate_weight[0], 0, 1), jnp.swapaxes(up_weight[0], 0, 1), down_weight[0]]
    )
    side = 4
    along_x = [[y + side * x for x in range(side)] for y in range(side)]
    along_y = [[side * x + y for y in range(side)] for x in range(side)]
    piece = lax.all_gather(weight_stack, "seq", axis=0, axis_index_groups=along_x)
    send_both = jnp.stack(
        [
            send_rows.reshape(n_exp, capacity, feature_width),
            send_grads.reshape(n_exp, capacity, feature_width),
        ],
        axis=1,
    )
    arrived = lax.all_to_all(send_both, "exp", split_axis=0, concat_axis=0, tiled=True)
    arrived = jnp.swapaxes(arrived, 0, 1).reshape(2, slot_count, feature_width)
    gathered = lax.all_gather(arrived, "seq", axis=0, axis_index_groups=along_y)
    rows_in = gathered[:, 0].reshape(side * slot_count, feature_width)
    grads_in = gathered[:, 1].reshape(side * slot_count, feature_width)
    gate_part, up_part, down_part = piece[:, 0], piece[:, 1], piece[:, 2]
    gate_pre = jnp.einsum("rd,kfd->krf", rows_in, gate_part, preferred_element_type=jnp.float32)
    up_pre = jnp.einsum("rd,kfd->krf", rows_in, up_part, preferred_element_type=jnp.float32)
    grad_hidden = jnp.einsum("rd,kfd->krf", grads_in, down_part, preferred_element_type=jnp.float32)
    sigma = jax.nn.sigmoid(gate_pre)
    silu_gate = gate_pre * sigma
    grad_gate_pre = (grad_hidden * up_pre * sigma * (1.0 + gate_pre * (1.0 - sigma))).astype(
        jnp.bfloat16
    )
    grad_up_pre = (grad_hidden * silu_gate).astype(jnp.bfloat16)
    back_term = jnp.einsum(
        "krf,kfd->rd", grad_gate_pre, gate_part, preferred_element_type=jnp.float32
    )
    back_term = back_term + jnp.einsum(
        "krf,kfd->rd", grad_up_pre, up_part, preferred_element_type=jnp.float32
    )
    back_term = back_term.astype(jnp.bfloat16).reshape(side, slot_count, feature_width)
    folded = lax.psum_scatter(
        back_term, "seq", scatter_dimension=0, axis_index_groups=along_y, tiled=False
    )
    slot_source = folded.reshape(n_exp, capacity, feature_width)
    slot_backs = lax.all_to_all(slot_source, "exp", split_axis=0, concat_axis=0, tiled=True)
    slot_backs = slot_backs.reshape(slot_count, feature_width)
    grad_normed = jnp.dot(member16, slot_backs, preferred_element_type=jnp.float32)
    grad_tokens = pullback(grad_normed)[0]
    return grad_tokens.astype(jnp.bfloat16).reshape(img_local, patch_local, feature_width)


def solution(mesh):
    in_specs = (
        P("exp", "seq", None),
        P("exp"),
        P(),
        P("exp", "seq", None, None),
        P("exp", "seq", None),
        P("exp", None, "seq"),
        P("exp", None, "seq"),
        P("exp", "seq", None),
        P("exp", "seq", None),
    )
    out_specs = P("exp", "seq", None)
    return jax.shard_map(
        per_device, mesh=mesh, in_specs=in_specs, out_specs=out_specs, check_vma=False
    )
```

time: 320 us -> 331 us (1.034)
  waiting for transfers between devices: 163 us -> 192 us
  matrix products: 73.1 us -> 51.3 us
  local copies, waits for them, and re-layouts: 6.47 us -> 14.6 us
  blocking collectives: 47.3 us -> 42.8 us
    reduce_scatter x0 -> x1, waiting for transfers between devices: none -> 36.9 us  [per_device(): lax.psum_scatter(back_term, 'seq', scatter_dimension=0, axis_index_groups...]
    dot_general x7, matrix products: 72.9 us -> 51.1 us  [the longest x1 20.5 us: per_device(): jnp.einsum('krf,kfd->rd', grad_gate_pre, gate_part, preferred_element_typ...]
    all_gather x1 -> x2, waiting for transfers between devices: 138 us -> 131 us  [the longest x1 79.3 us: per_device(): lax.all_gather(weight_stack, 'seq', axis=0, axis_index_groups=along_x)]
    slice x1 -> x2, local copies, waits for them, and re-layouts: 0.18 us -> 5.28 us  [the longest x1 5.09 us: per_device(): grads_in = gathered[:, 1].reshape(side * slot_count, feature_width)]
    another operation x3 -> x6, local copies, waits for them, and re-layouts: 1.29 us -> 6.3 us  [the longest x3 2.85 us: per_device(): jnp.stack([send_rows.reshape(n_exp, capacity, feature_width), send_grads....]
    all_to_all x1, blocking collectives: 47.3 us -> 42.8 us  [per_device(): lax.all_to_all(send_both, 'exp', split_axis=0, concat_axis=0, tiled=True)]
  transfers between devices with their start and end apart: 2 -> 4, of which waited for: 2 -> 4; matrix products, arithmetic and copies ran while one was open for 4% -> 2% of each run, Pallas kernels for 0% -> 0%
where the time goes in v1:
time: 331 us; the launch traced here: 330 us
  waiting for transfers between devices  192 us (58%)
  matrix products  51.3 us (15%)
  blocking collectives  42.8 us (13%)
  local copies, waits for them, and re-layouts  14.6 us (4%)
  between operations  13.3 us (4%)
  other arithmetic  8.08 us (2%)
  starting transfers between devices  8.02 us (2%)
    all_gather x1, waiting for transfers between devices, per_device(): lax.all_gather(weight_stack, 'seq', axis=0, axis_index_groups=along_x)  79.3 us
    all_gather x1, waiting for transfers between devices, per_device(): gathered = lax.all_gather(arrived, 'seq', axis=0, axis_index_groups=along_y)  51.4 us
    all_to_all x1, blocking collectives, per_device(): lax.all_to_all(send_both, 'exp', split_axis=0, concat_axis=0, tiled=True)  42.8 us
    reduce_scatter x1, waiting for transfers between devices, per_device(): lax.psum_scatter(back_term, 'seq', scatter_dimension=0, axis_index_groups...  36.9 us
    all_to_all x1, waiting for transfers between devices, per_device(): lax.all_to_all(slot_source, 'exp', split_axis=0, concat_axis=0, tiled=True)  24.6 us
    dot_general x1, matrix products, per_device(): jnp.einsum('krf,kfd->rd', grad_gate_pre, gate_part, preferred_element_typ...  20.5 us
    dot_general x1, matrix products, per_device(): jnp.einsum('krf,kfd->rd', grad_up_pre, up_part, preferred_element_type=jn...  11.6 us
    dot_general x1, matrix products, per_device(): jnp.einsum('rd,kfd->krf', grads_in, down_part, preferred_element_type=jnp...  8.96 us
  transfers between devices with their start and end apart: 4, of which 4 were waited for; matrix products, arithmetic and copies ran while one was open for 2% of the time, Pallas kernels for 0%

profile of v1, /device:TPU:1, one launch (start us, length us, event | category | flops | bytes accessed | tf_op | source)
XLA Modules:
  0.0 330.3 jit_solution(3287927629950372840)
XLA Ops:
  6.5 0.7 convert_reduce_fusion.1
  7.3 0.7 convert_element_type.66
  8.0 0.7 broadcast_multiply_fusion
  8.7 0.8 copy.51
  9.8 1.1 fusion.18
  12.3 1.0 copy.69
  14.6 1.2 convolution_convert_fusion
  15.8 1.3 stack_reshape.6
  17.3 1.3 copy.57
  18.7 42.8 %all_to_all.10 = bf16[16,2,17,1152]{3,1,2,0:T(2,128)(2,1)S(1)} all-to-all(bf16[16,2,17,1152]{3,1,2,0:T(2,128)(2,1)S(1)} %copy.57), channel_id=1, replica_groups=mesh['seq'=16,'exp'=16] {'exp'}, dimensions={0} | all-to-all | bytes 2506752 | tf_op jit(solution)/shard_map/all_to_all | solution.py:91
  61.5 1.2 copy.58
  62.8 2.6 pad_maximum_fusion
  65.6 51.4 %all-gather.4.cloned.1.call-done = bf16[4,2,272,1152]{3,2,1,0:T(8,128)(2,1)} async-done(((bf16[1,2,272,1152]{3,2,1,0:T(8,128)(2,1)}), bf16[4,2,272,1152]{3,2,1,0:T(8,128)(2,1)}) %all-gather.4.cloned.1.call-update) | async-done | bytes 5013520 | tf_op jit(solution)/shard_map/all_gather | solution.py:93
  117.1 5.1 %fusion.35 = (bf16[4,1,272,1152]{3,2,1,0:T(8,128)(2,1)}, bf16[4,1,272,1152]{3,2,1,0:T(8,128)(2,1)}) fusion(bf16[4,2,272,1152]{3,2,1,0:T(8,128)(2,1)} %all-gather.4.cloned.1.call-done), kind=kLoop, calls=%fused_computation.70 | loop fusion | bytes 10027008 | tf_op jit(solution)/shard_map/slice | solution.py:95
  122.1 79.3 %all-gather.6.cloned.1.call-done = bf16[12,288,1152]{2,1,0:T(8,128)(2,1)} async-done(((bf16[3,288,1152]{2,1,0:T(8,128)(2,1)}), bf16[12,288,1152]{2,1,0:T(8,128)(2,1)}) %all-gather.6.cloned.1.call-update) | async-done | bytes 7962640 | tf_op jit(solution)/shard_map/all_gather | solution.py:83
  201.4 9.0 %fusion.12 = f32[4,288,1088]{2,1,0:T(8,128)} fusion(bf16[1088,1152,1]{1,0,2:T(8,128)(2,1)} %bitcast.154, bf16[4,3,288,1152]{3,2,1,0:T(8,128)(2,1)} %bitcast.160), kind=kOutput, calls=%fused_computation.21 | convolution fusion | flops 2887778304 | bytes 10174464 | tf_op jit(solution)/shard_map/rd,kfd->krf/dot_general | solution.py:99
  210.4 8.0 %fusion.15 = f32[4,288,1088]{2,1,0:T(8,128)} fusion(bf16[1088,1152,1]{1,0,2:T(8,128)(2,1)S(1)} %bitcast.153, bf16[4,3,288,1152]{3,2,1,0:T(8,128)(2,1)} %bitcast.161), kind=kOutput, calls=%fused_computation.26 | convolution fusion | flops 2887778304 | bytes 10174464 | tf_op jit(solution)/shard_map/rd,kfd->krf/dot_general | solution.py:97
  218.4 20.5 %convolution_bitcast_fusion.1 = f32[1088,1152]{1,0:T(8,128)} fusion(bf16[4,3,288,1152]{3,2,1,0:T(8,128)(2,1)} %bitcast.162, f32[4,288,1088]{2,1,0:T(8,128)} %fusion.15, f32[4,288,1088]{2,1,0:T(8,128)} %fusion.12, bf16[1088,1152,1]{1,0,2:T(8,128)(2,1)} %bitcast.152), kind=kOutput, calls=%fused_computation.2 | convolution fusion | flops 5788090368 | bytes 23445504 | tf_op jit(solution)/shard_map/krf,kfd->rd/dot_general | solution.py:106
  238.9 11.6 %fusion.1 = bf16[1088,1152]{1,0:T(8,128)(2,1)} fusion(f32[1088,1152]{1,0:T(8,128)} %convolution_bitcast_fusion.1, f32[4,288,1088]{2,1,0:T(8,128)} %fusion.15, f32[4,288,1088]{2,1,0:T(8,128)} %fusion.12, bf16[4,3,288,1152]{3,2,1,0:T(8,128)(2,1)} %bitcast.163), kind=kOutput, calls=%fused_computation.3 | convolution fusion | flops 2897805312 | bytes 20791296 | tf_op jit(solution)/shard_map/krf,kfd->rd/dot_general | solution.py:109
  250.5 36.9 %reduce-scatter.2.cloned.1.call-done = bf16[1,272,1152]{2,1,0:T(8,128)(2,1)} async-done(((bf16[4,272,1152]{2,1,0:T(8,128)(2,1)}), bf16[1,272,1152]{2,1,0:T(8,128)(2,1)}) %reduce-scatter.2.cloned.1.call-update) | async-done | bytes 626704 | tf_op jit(solution)/shard_map/reduce_scatter | solution.py:113
  287.5 2.2 reshape_reduce_scatter.3
  289.7 7.8 %all-to-all-start.1 = ((bf16[16,17,1152]{2,1,0:T(8,128)(2,1)}), bf16[16,17,1152]{2,1,0:T(8,128)(2,1)S(1)}, u32[]{:S(2)}, u32[]{:S(2)}) async-start(bf16[16,17,1152]{2,1,0:T(8,128)(2,1)} %reshape_reduce_scatter.3), calls=%async_computation.2 | async-start | bytes 1769472 | tf_op jit(solution)/shard_map/all_to_all | solution.py:117
  297.5 24.6 %all-to-all-done.1 = bf16[16,17,1152]{2,1,0:T(8,128)(2,1)S(1)} async-done(((bf16[16,17,1152]{2,1,0:T(8,128)(2,1)}), bf16[16,17,1152]{2,1,0:T(8,128)(2,1)S(1)}, u32[]{:S(2)}, u32[]{:S(2)}) %all-to-all-start.1) | async-done | bytes 626720 | tf_op jit(solution)/shard_map/all_to_all | solution.py:117
  322.9 0.9 fusion.16
  (53 shorter events, 4.4 us)
Async XLA Ops:
  6.5 7.0 %copy-start = (bf16[2,64,1152]{2,1,0:T(8,128)(2,1)S(1)}, bf16[2,64,1152]{2,1,0:T(8,128)(2,1)}, u32[]{:S(2)}) copy-start(bf16[2,64,1152]{2,1,0:T(8,128)(2,1)} %param.17) | copy-start | bytes 884740
  6.5 7.5 %copy-start.7 = (s32[2]{0:T(128)S(1)}, s32[2]{0:T(128)}, u32[]{:S(2)}) copy-start(s32[2]{0:T(128)} %param.10) | copy-start | bytes 28
  6.5 110.5 %all-gather.4.cloned.1.call-start = ((), (), s32[]{:S(2)}) async-start(), calls=%async_computation.3 | async-start | bytes 6266880 | tf_op jit(solution)/shard_map/all_gather | solution.py:93
  9.6 4.8 %copy-start.1 = (bf16[2,64,1152]{2,1,0:T(8,128)(2,1)S(1)}, bf16[2,64,1152]{2,1,0:T(8,128)(2,1)}, u32[]{:S(2)}) copy-start(bf16[2,64,1152]{2,1,0:T(8,128)(2,1)} %param.9) | copy-start | bytes 884740
  13.5 1.1 copy-start.3
  18.7 44.1 %copy-start.5 = (bf16[1,288,1152]{2,1,0:T(8,128)(2,1)S(1)}, bf16[1,288,1152]{2,1,0:T(8,128)(2,1)}, u32[]{:S(2)}) copy-start(bf16[1,288,1152]{2,1,0:T(8,128)(2,1)} %param.16) | copy-start | bytes 1990660
  18.7 44.1 %copy-start.6 = (bf16[1,1152,288]{1,2,0:T(8,128)(2,1)S(1)}, bf16[1,1152,288]{1,2,0:T(8,128)(2,1)}, u32[]{:S(2)}) copy-start(bf16[1,1152,288]{1,2,0:T(8,128)(2,1)} %param.15) | copy-start | bytes 1990660
  62.7 138.7 %all-gather.6.cloned.1.call-start = ((), (), s32[]{:S(2)}) async-start(), calls=%async_computation.5 | async-start | bytes 9953280 | tf_op jit(solution)/shard_map/all_gather | solution.py:83
  65.4 222.0 %reduce-scatter.2.cloned.1.call-start = ((), (), s32[]{:S(2)}) async-start(), calls=%async_computation.4 | async-start | bytes 3133440 | tf_op jit(solution)/shard_map/reduce_scatter | solution.py:113
  201.4 9.0 %copy-start.2 = (bf16[4,1,272,1152]{3,2,1,0:T(8,128)(2,1)S(1)}, bf16[4,1,272,1152]{3,2,1,0:T(8,128)(2,1)}, u32[]{:S(2)}) copy-start(bf16[4,1,272,1152]{3,2,1,0:T(8,128)(2,1)} %get-tuple-element.8) | copy-start | bytes 7520260
  250.5 71.8 %copy-start.4 = (bf16[128,272]{0,1:T(8,128)(2,1)S(1)}, bf16[128,272]{0,1:T(8,128)(2,1)}, u32[]{:S(2)}) copy-start(bf16[128,272]{0,1:T(8,128)(2,1)} %copy-done.3) | copy-start | bytes 208900
  289.7 32.5 %all-to-all-start.1 = ((bf16[16,17,1152]{2,1,0:T(8,128)(2,1)}), bf16[16,17,1152]{2,1,0:T(8,128)(2,1)S(1)}, u32[]{:S(2)}, u32[]{:S(2)}) async-start(bf16[16,17,1152]{2,1,0:T(8,128)(2,1)} %reshape_reduce_scatter.3), calls=%async_computation.2 | async-start | bytes 1769472 | tf_op jit(solution)/shard_map/all_to_all | solution.py:117
Sparse Core Ops, SparseCore 0:
  62.8 54.1 all-gather.3
  118.9 82.5 all-gather.5
  250.6 36.7 reduce-scatter.1

commit v2 on v1

v2 whole, which is shorter than its diff:
```python
import functools

import jax
import jax.numpy as jnp
from jax import lax
from jax.experimental import pallas as pl
from jax.experimental.pallas import tpu as pltpu
from jax.sharding import PartitionSpec as P

MESH = pl.DeviceIdType.MESH
NT = (((1,), (1,)), ((), ()))
NN = (((1,), (0,)), ((), ()))
SIDE = 4
TILE = 16


def normalize_modulate(tokens_f, shift, scale):
    mean_square = jnp.mean(tokens_f * tokens_f, axis=-1, keepdims=True)
    return tokens_f / jnp.sqrt(mean_square + 1e-06) * (1.0 + scale) + shift


def z_offsets(nz):
    order = [0]
    for step in range(1, nz):
        for way in (step, nz - step):
            if way not in order:
                order.append(way)
    return order


def expert_kernel(
    nz,
    w_ref,
    xm_ref,
    xe_ref,
    om_ref,
    oe_ref,
    wbuf,
    tbuf,
    ebuf,
    acc,
    pbuf,
    relay_a,
    relay_b,
    in_r,
    in_l,
    fbuf,
    febuf,
    w_loc,
    w_send,
    w_recv,
    wf_send,
    wf_recv,
    d_send,
    d_recv,
    e_send,
    e_recv,
    t_send,
    t_recv,
    tf_send,
    tf_recv,
    r_send,
    r_recv,
    o_send,
    o_recv,
    oe_send,
    oe_recv,
):
    n_exp = 2 * nz
    chunks = n_exp + 1
    width = w_ref.shape[-1]
    half = w_ref.shape[2]
    rows_count = chunks * TILE
    cut = (chunks + 1) // 2 * TILE
    hidden = SIDE * 2 * half
    early = 3 * 2 * half

    s = lax.axis_index("seq")
    e = lax.axis_index("exp")
    core = lax.rem(e, 2)
    z = lax.div(e, 2)
    hi = lax.div(s, SIDE)
    lo = lax.rem(s, SIDE)
    w_at = (1 - core) * hi + core * lo
    t_at = (1 - core) * lo + core * hi
    w_step = SIDE - (SIDE - 1) * core
    t_step = 1 + (SIDE - 1) * core

    def on_w(offset):
        return (lax.rem(w_at + offset, SIDE) * w_step + t_at * t_step, e)

    def on_t(offset):
        return (w_at * w_step + lax.rem(t_at + offset, SIDE) * t_step, e)

    w_right, w_left = on_w(1), on_w(SIDE - 1)
    t_right, t_left = on_t(1), on_t(SIDE - 1)

    offsets = [(dz, dc) for dz in z_offsets(nz) for dc in (0, 1)]

    def peer(k, sign):
        dz, dc = offsets[k]
        if sign < 0:
            dz = (nz - dz) % nz
        return lax.rem(z + dz, nz) * 2 + lax.rem(core + dc, 2)

    def remote(src, dst, send, recv, device):
        return pltpu.make_async_remote_copy(
            src_ref=src,
            dst_ref=dst,
            send_sem=send,
            recv_sem=recv,
            device_id=device,
            device_id_type=MESH,
        )

    barrier = pltpu.get_barrier_semaphore()
    greeted = [w_right, w_left, t_right, t_left] + [(s, peer(k, 1)) for k in range(1, n_exp)]
    for device in greeted:
        pl.semaphore_signal(barrier, inc=1, device_id=device, device_id_type=MESH)
    pl.semaphore_wait(barrier, len(greeted))

    pieces = [(m, h) for m in range(3) for h in range(2)]
    w_right_copy = {}
    w_left_copy = {}
    for m, h in pieces:
        w_right_copy[m, h] = remote(
            w_ref.at[m, h],
            wbuf.at[m, 1, h],
            w_send.at[0, 2 * m + h],
            w_recv.at[0, 2 * m + h],
            w_right,
        )
        w_left_copy[m, h] = remote(
            w_ref.at[m, h],
            wbuf.at[m, 2, h],
            w_send.at[1, 2 * m + h],
            w_recv.at[1, 2 * m + h],
            w_left,
        )
    local = [
        pltpu.make_async_copy(w_ref.at[m, h], wbuf.at[m, 0, h], w_loc.at[2 * m + h])
        for m, h in pieces
    ]
    local.append(pltpu.make_async_copy(xm_ref.at[e], tbuf.at[0, 0], d_recv.at[0]))
    local.append(pltpu.make_async_copy(xe_ref.at[e], ebuf.at[0], e_recv.at[0]))
    for copy in local:
        copy.start()
    d_copy = [local[-2]]
    e_copy = [local[-1]]
    for k in range(1, n_exp):
        there = peer(k, 1)
        d_copy.append(
            remote(xm_ref.at[there], tbuf.at[0, k], d_send.at[k], d_recv.at[k], (s, there))
        )
        e_copy.append(
            remote(xe_ref.at[there], ebuf.at[k], e_send.at[k], e_recv.at[k], (s, there))
        )
    for k in range(1, n_exp):
        d_copy[k].start()
        e_copy[k].start()
    for m in range(3):
        w_right_copy[m, 0].start()
        w_left_copy[m, 1].start()
    for m in range(3):
        w_right_copy[m, 1].start()
        w_left_copy[m, 0].start()

    acc[...] = jnp.zeros_like(acc)

    wf_right = [
        remote(wbuf.at[m, 1, 0], wbuf.at[m, 3, 0], wf_send.at[0, m], wf_recv.at[0, m], w_right)
        for m in range(3)
    ]
    wf_left = [
        remote(wbuf.at[m, 2, 1], wbuf.at[m, 3, 1], wf_send.at[1, m], wf_recv.at[1, m], w_left)
        for m in range(3)
    ]
    tr_copy = [
        remote(tbuf.at[0, i], tbuf.at[1, i], t_send.at[0, i], t_recv.at[0, i], t_right)
        for i in range(chunks)
    ]
    tl_copy = [
        remote(tbuf.at[0, i], tbuf.at[2, i], t_send.at[1, i], t_recv.at[1, i], t_left)
        for i in range(chunks)
    ]
    tf_copy = [
        remote(
            tbuf.at[1 + i % 2, i],
            tbuf.at[3, i],
            tf_send.at[i],
            tf_recv.at[i],
            t_left if i % 2 else t_right,
        )
        for i in range(chunks)
    ]

    def pass_on(i):
        tr_copy[i].wait_recv()
        tl_copy[i].wait_recv()
        tf_copy[i].start()

    lag = 2
    for i in range(chunks):
        if i < n_exp:
            if i == 0:
                d_copy[i].wait()
            else:
                d_copy[i].wait_recv()
        else:
            e_copy[0].wait()
            for k in range(1, n_exp):
                e_copy[k].wait_recv()
            tbuf[0, n_exp, 0:TILE, :] = ebuf[:, 0, :].astype(jnp.bfloat16)
            tbuf[0, n_exp, TILE : 2 * TILE, :] = ebuf[:, 1, :].astype(jnp.bfloat16)
        tr_copy[i].start()
        tl_copy[i].start()
        if i in (2, 4, 6):
            m = i // 2 - 1
            w_right_copy[m, 0].wait_recv()
            wf_right[m].start()
            w_left_copy[m, 1].wait_recv()
            wf_left[m].start()
        if i >= lag:
            pass_on(i - lag)
    for i in range(chunks - lag, chunks):
        pass_on(i)
    for copy in local[: len(pieces)]:
        copy.wait()
    for m in range(3):
        w_right_copy[m, 1].wait_recv()
        w_left_copy[m, 0].wait_recv()

    def weights(m, start, size):
        flat = wbuf.at[m].reshape(hidden, width)
        return flat[pl.ds(start, size), :]

    def add_chunk(slot, start, size):
        rows = tbuf[slot, :, 0:TILE, :].reshape(rows_count, width)
        grads = tbuf[slot, :, TILE : 2 * TILE, :].reshape(rows_count, width)
        gate = weights(0, start, size)
        up = weights(1, start, size)
        down = weights(2, start, size)
        gate_pre = lax.dot_general(rows, gate, NT, preferred_element_type=jnp.float32)
        up_pre = lax.dot_general(rows, up, NT, preferred_element_type=jnp.float32)
        grad_hidden = lax.dot_general(grads, down, NT, preferred_element_type=jnp.float32)
        sigma = 1.0 / (1.0 + jnp.exp(-gate_pre))
        scaled = grad_hidden * sigma
        grad_gate = (scaled * up_pre * (1.0 + gate_pre * (1.0 - sigma))).astype(jnp.bfloat16)
        grad_up = (scaled * gate_pre).astype(jnp.bfloat16)
        back = lax.dot_general(grad_gate, gate, NN, preferred_element_type=jnp.float32)
        back += lax.dot_general(grad_up, up, NN, preferred_element_type=jnp.float32)
        acc[slot] += back

    first = early // 2

    def early_chunk(n, carry):
        slot = lax.div(n, 2)

        @pl.when(n == 6)
        def _():
            for m in range(3):
                wf_right[m].wait_recv()
                wf_left[m].wait_recv()
            for i in range(chunks):
                tf_copy[i].wait_recv()

        add_chunk(slot, pl.multiple_of(lax.rem(n, 2) * first, TILE), first)
        return carry

    lax.fori_loop(0, 8, early_chunk, 0)

    def rounded(slot, lower, upper):
        return acc[slot, lower:upper, :].astype(jnp.bfloat16)

    half_a, half_b = pl.ds(0, cut), pl.ds(cut, rows_count - cut)
    ra = remote(pbuf.at[0, half_a], relay_a, r_send.at[0], r_recv.at[0], t_left)
    rb = remote(pbuf.at[0, half_b], relay_b, r_send.at[1], r_recv.at[1], t_right)
    la = remote(pbuf.at[1, half_a], in_r.at[half_a], r_send.at[2], r_recv.at[2], t_left)
    lb = remote(pbuf.at[1, half_b], in_r.at[half_b], r_send.at[3], r_recv.at[3], t_left)
    xa = remote(pbuf.at[2, half_a], in_l.at[half_a], r_send.at[4], r_recv.at[4], t_right)
    xb = remote(pbuf.at[2, half_b], in_l.at[half_b], r_send.at[5], r_recv.at[5], t_right)

    add_chunk(3, early, hidden - early)
    pbuf[0] = rounded(3, 0, rows_count)
    ra.start()
    rb.start()

    add_chunk(1, early, hidden - early)
    pbuf[1, cut:, :] = rounded(1, cut, rows_count)
    lb.start()
    ra.wait_recv()
    pbuf[1, 0:cut, :] = (acc[1, 0:cut, :] + relay_a[...].astype(jnp.float32)).astype(jnp.bfloat16)
    la.start()

    add_chunk(2, early, hidden - early)
    pbuf[2, 0:cut, :] = rounded(2, 0, cut)
    xa.start()
    rb.wait_recv()
    pbuf[2, cut:, :] = (acc[2, cut:, :] + relay_b[...].astype(jnp.float32)).astype(jnp.bfloat16)
    xb.start()

    add_chunk(0, early, hidden - early)
    for copy in (la, lb, xa, xb):
        copy.wait_recv()
    total = acc[0] + in_r[...].astype(jnp.float32) + in_l[...].astype(jnp.float32)
    total = total.astype(jnp.bfloat16)
    fbuf[...] = total.reshape(chunks, TILE, width)
    febuf[:, 0, :] = total[n_exp * TILE :, :].astype(jnp.float32)

    mine = pltpu.make_async_copy(fbuf.at[0], om_ref.at[e], o_recv.at[0])
    mine_e = pltpu.make_async_copy(febuf.at[0], oe_ref.at[e], oe_recv.at[0])
    o_copy, oe_copy = [], []
    for k in range(1, n_exp):
        there = peer(k, -1)
        o_copy.append(
            remote(fbuf.at[k], om_ref.at[e], o_send.at[k], o_recv.at[k], (s, there))
        )
        oe_copy.append(
            remote(febuf.at[k], oe_ref.at[e], oe_send.at[k], oe_recv.at[k], (s, there))
        )
    for k in range(n_exp - 2, -1, -1):
        o_copy[k].start()
        oe_copy[k].start()
    mine.start()
    mine_e.start()

    for group in (
        w_right_copy.values(),
        w_left_copy.values(),
        wf_right,
        wf_left,
        d_copy[1:],
        e_copy[1:],
        tr_copy,
        tl_copy,
        tf_copy,
        (ra, rb, la, lb, xa, xb),
    ):
        for copy in group:
            copy.wait_send()
    mine.wait()
    mine_e.wait()
    for k in range(1, n_exp):
        here = peer(k, 1)
        o_copy[k - 1].wait_send()
        oe_copy[k - 1].wait_send()
        remote(
            fbuf.at[k], om_ref.at[here], o_send.at[k], o_recv.at[k], (s, here)
        ).wait_recv()
        remote(
            febuf.at[k], oe_ref.at[here], oe_send.at[k], oe_recv.at[k], (s, here)
        ).wait_recv()


def run_experts(weights, send_main, send_extra):
    n_exp, _, width = send_main.shape
    half = weights.shape[2]
    chunks = n_exp + 1
    rows_count = chunks * TILE
    cut = (chunks + 1) // 2 * TILE
    bf16, f32 = jnp.bfloat16, jnp.float32
    dma = pltpu.SemaphoreType.DMA
    anywhere = pl.BlockSpec(memory_space=pl.ANY)
    return pl.pallas_call(
        functools.partial(expert_kernel, n_exp // 2),
        out_shape=(
            jax.ShapeDtypeStruct((n_exp, TILE, width), bf16),
            jax.ShapeDtypeStruct((n_exp, 1, width), f32),
        ),
        in_specs=[anywhere] * 3,
        out_specs=(anywhere, anywhere),
        scratch_shapes=[
            pltpu.VMEM((3, SIDE, 2, half, width), bf16),
            pltpu.VMEM((SIDE, chunks, 2 * TILE, width), bf16),
            pltpu.VMEM((n_exp, 2, width), f32),
            pltpu.VMEM((SIDE, rows_count, width), f32),
            pltpu.VMEM((3, rows_count, width), bf16),
            pltpu.VMEM((cut, width), bf16),
            pltpu.VMEM((rows_count - cut, width), bf16),
            pltpu.VMEM((rows_count, width), bf16),
            pltpu.VMEM((rows_count, width), bf16),
            pltpu.VMEM((chunks, TILE, width), bf16),
            pltpu.VMEM((n_exp, 1, width), f32),
            dma((6,)),
            dma((2, 6)),
            dma((2, 6)),
            dma((2, 3)),
            dma((2, 3)),
            dma((n_exp,)),
            dma((n_exp,)),
            dma((n_exp,)),
            dma((n_exp,)),
            dma((2, chunks)),
            dma((2, chunks)),
            dma((chunks,)),
            dma((chunks,)),
            dma((6,)),
            dma((6,)),
            dma((n_exp,)),
            dma((n_exp,)),
            dma((n_exp,)),
            dma((n_exp,)),
        ],
        compiler_params=pltpu.CompilerParams(
            collective_id=0, has_side_effects=True, vmem_limit_bytes=60 * 2**20
        ),
        name="experts",
    )(weights, send_main, send_extra)


def per_device(
    tokens,
    timesteps,
    modulation,
    routes,
    gate_codes,
    gate_weight,
    up_weight,
    down_weight,
    cotangent,
):
    img_local, patch_local, feature_width = tokens.shape
    top_count = routes.shape[3]
    row_count = img_local * patch_local
    n_exp = lax.axis_size("exp")
    block_width = gate_weight.shape[2]
    level_count = modulation.shape[0]
    select = (timesteps[:, None] == jnp.arange(level_count, dtype=jnp.int32)[None, :]).astype(
        jnp.float32
    )
    table = jnp.dot(
        select,
        modulation.astype(jnp.float32).reshape(level_count, 2 * feature_width),
        precision=lax.Precision.HIGHEST,
    )
    table = jnp.broadcast_to(
        table[:, None, :], (img_local, patch_local, 2 * feature_width)
    ).reshape(row_count, 2 * feature_width)
    scale = table[:, :feature_width]
    shift = table[:, feature_width:]
    tokens_f = tokens.reshape(row_count, feature_width).astype(jnp.float32)
    pre, pullback = jax.vjp(lambda value: normalize_modulate(value, shift, scale), tokens_f)
    normed = pre.astype(jnp.bfloat16)
    codes = gate_codes.reshape(row_count, top_count).astype(jnp.float32)
    route_weight = codes / jnp.sum(codes, axis=-1, keepdims=True)
    flat_routes = jnp.transpose(routes[0], (1, 0, 2)).reshape(row_count * top_count)
    expert_hot = (
        flat_routes[:, None] == jnp.arange(n_exp, dtype=jnp.int32)[None, :]
    ).astype(jnp.int32)
    earlier = jnp.cumsum(expert_hot, axis=0) - expert_hot
    position = jnp.sum(earlier * expert_hot, axis=1)
    slot_ids = jnp.where(
        position < TILE, flat_routes * TILE + position, n_exp * TILE + flat_routes
    )
    slot_count = n_exp * (TILE + 1)
    slot_hot = (slot_ids[:, None] == jnp.arange(slot_count, dtype=jnp.int32)[None, :]).astype(
        jnp.float32
    )
    slot_hot = slot_hot.reshape(row_count, top_count, slot_count)
    member = jnp.sum(slot_hot, axis=1).astype(jnp.bfloat16)
    slot_weight = jnp.sum(slot_hot * route_weight[:, :, None], axis=(0, 1))
    contract_tokens = (((0,), (0,)), ((), ()))
    send_rows = lax.dot_general(
        member, normed, contract_tokens, preferred_element_type=jnp.float32
    ).astype(jnp.bfloat16)
    picked = lax.dot_general(
        member,
        cotangent.reshape(row_count, feature_width),
        contract_tokens,
        preferred_element_type=jnp.float32,
    )
    send_grads = (picked * slot_weight[:, None]).astype(jnp.bfloat16)
    main = n_exp * TILE
    send_main = jnp.concatenate(
        [
            send_rows[:main].reshape(n_exp, TILE, feature_width),
            send_grads[:main].reshape(n_exp, TILE, feature_width),
        ],
        axis=1,
    )
    send_extra = jnp.stack([send_rows[main:], send_grads[main:]], axis=1).astype(jnp.float32)
    weights = jnp.stack(
        [jnp.swapaxes(gate_weight[0], 0, 1), jnp.swapaxes(up_weight[0], 0, 1), down_weight[0]]
    ).reshape(3, 2, block_width // 2, feature_width)
    back_main, back_extra = run_experts(weights, send_main, send_extra)
    slot_backs = jnp.concatenate(
        [
            back_main.reshape(main, feature_width),
            back_extra.reshape(n_exp, feature_width).astype(jnp.bfloat16),
        ]
    )
    grad_normed = jnp.dot(member, slot_backs, preferred_element_type=jnp.float32)
    grad_tokens = pullback(grad_normed)[0]
    return grad_tokens.astype(jnp.bfloat16).reshape(img_local, patch_local, feature_width)


def solution(mesh):
    in_specs = (
        P("exp", "seq", None),
        P("exp"),
        P(),
        P("exp", "seq", None, None),
        P("exp", "seq", None),
        P("exp", None, "seq"),
        P("exp", None, "seq"),
        P("exp", "seq", None),
        P("exp", "seq", None),
    )
    out_specs = P("exp", "seq", None)
    return jax.shard_map(
        per_device, mesh=mesh, in_specs=in_specs, out_specs=out_specs, check_vma=False
    )
```

time: 331 us -> 128 us (0.39)
  waiting for transfers between devices: 192 us -> 0 us
  Pallas kernels: 0 us -> 110 us
  matrix products: 51.3 us -> 2.44 us
  blocking collectives: 42.8 us -> 0 us
  between operations: 13.3 us -> 0.2 us
  local copies, waits for them, and re-layouts: 14.6 us -> 4.94 us
  starting transfers between devices: 8.02 us -> 0 us
    all_gather x2 -> x0, waiting for transfers between devices: 131 us -> none  [the longest x1 79.3 us: per_device(): lax.all_gather(weight_stack, 'seq', axis=0, axis_index_groups=along_x)]
    pallas_call x0 -> x1, Pallas kernels: none -> 110 us  [run_experts(): pl.pallas_call(functools.partial(expert_kernel, n_exp // 2), out_shape=(j...]
    dot_general x7 -> x3, matrix products: 51.1 us -> 2.23 us  [the longest x1 1.55 us: per_device(): jnp.dot(member, slot_backs, preferred_element_type=jnp.float32)]
    all_to_all x1 -> x0, blocking collectives: 42.8 us -> none  [per_device(): lax.all_to_all(send_both, 'exp', split_axis=0, concat_axis=0, tiled=True)]
    reduce_scatter x1 -> x0, waiting for transfers between devices: 36.9 us -> none  [per_device(): lax.psum_scatter(back_term, 'seq', scatter_dimension=0, axis_index_groups...]
    all_to_all x1 -> x0, waiting for transfers between devices: 24.6 us -> none  [per_device(): lax.all_to_all(slot_source, 'exp', split_axis=0, concat_axis=0, tiled=True)]
    all_to_all x1 -> x0, starting transfers between devices: 7.76 us -> none  [per_device(): lax.all_to_all(slot_source, 'exp', split_axis=0, concat_axis=0, tiled=True)]
    another operation x6 -> x5, local copies, waits for them, and re-layouts: 6.3 us -> 0.13 us  [the longest x4 0.13 us: per_device(): jnp.stack([send_rows[main:], send_grads[main:]], axis=1).astype(jnp.float32)]
  transfers between devices with their start and end apart: 4 -> 0, of which waited for: 4 -> 0; matrix products, arithmetic and copies ran while one was open for 2% -> 0% of each run, Pallas kernels for 0% -> 0%
where the time goes in v2:
time: 128 us
  Pallas kernels  110 us (86%)
  other arithmetic  9.67 us (8%)
  local copies, waits for them, and re-layouts  4.94 us (4%)
  matrix products  2.44 us (2%)
    pallas_call x1, Pallas kernels, run_experts(): pl.pallas_call(functools.partial(expert_kernel, n_exp // 2), out_shape=(j...  110 us

profile of v2, /device:TPU:1, one launch (start us, length us, event | category | flops | bytes accessed | tf_op | source)
XLA Modules:
  0.0 127.6 jit_solution(15425578681747617067)
XLA Ops:
  0.0 1.0 copy-done
  1.0 0.7 convert_reduce_fusion.1
  1.7 1.1 fusion.6
  3.0 0.7 convert_element_type.66
  3.8 0.7 broadcast_multiply_fusion
  4.6 0.8 copy.21
  5.7 0.6 reduce-window.6
  6.3 0.2 slice_reduce_fusion
  6.6 0.1 reduce_sum.61
  7.0 0.2 convert_reduce_fusion
  7.2 0.2 fusion.13
  7.4 0.3 fusion
  7.9 0.6 copy-done.2
  8.6 0.4 copy-done.1
  9.0 0.2 fusion.5
  9.2 0.3 convolution_convert_fusion
  9.6 0.6 slice-done
  10.2 1.1 pad_maximum_fusion.1.xm_ref
  11.4 0.8 maximum_convert_fusion.xe_ref
  12.3 1.5 %pad_maximum_fusion.w_ref = bf16[3,2,144,1152]{3,2,1,0:T(8,128)(2,1)} fusion(bf16[1,2,144,1152]{3,2,1,0:T(8,128)(2,1)S(1)} %bitcast.82, bf16[1,2,144,1152]{3,2,1,0:T(8,128)(2,1)S(1)} %bitcast.83, bf16[1,2,144,1152]{3,2,1,0:T(8,128)(2,1)S(1)} %bitcast.84), kind=kLoop, calls=%fused_computation.4 | loop fusion | flops 1990656 | bytes 3981312 | tf_op jit(solution)/shard_map/stack | solution.py:482
  13.8 110.4 %experts.1 = (bf16[16,16,1152]{2,1,0:T(8,128)(2,1)}, f32[16,1,1152]{2,1,0:T(1,128)}) custom-call(bf16[3,2,144,1152]{3,2,1,0:T(8,128)(2,1)} %pad_maximum_fusion.w_ref, bf16[16,32,1152]{2,1,0:T(8,128)(2,1)} %pad_maximum_fusion.1.xm_ref, f32[16,2,1152]{2,1,0:T(2,128)} %maximum_convert_fusion.xe_ref), custom_call_target="tpu_custom_call" | custom-call | tf_op jit(solution)/shard_map/experts/pallas_call | solution.py:364
  124.2 0.9 convert_element_type.70
  125.2 1.6 %fusion.8 = (f32[128]{0:T(128)S(1)}, f32[128,1152]{1,0:T(8,128)S(1)}) fusion(bf16[2,64,1152]{2,1,0:T(8,128)(2,1)S(1)} %copy-done.1, f32[128]{0:T(128)S(1)} %multiply_divide_fusion, f32[128,2304]{1,0:T(8,128)S(1)} %bitcast.78, bf16[128,272]{0,1:T(8,128)(2,1)S(1)} %get-tuple-element.9, bf16[16,1152]{1,0:T(8,128)(2,1)S(1)} %bitcast.87, ...), kind=kOutput, calls=%fused_computation.20 | convolution fusion | flops 82354048 | bytes 2171904 | tf_op jit(solution)/shard_map/dot_general | solution.py:492
  126.7 0.9 fusion.4
  (41 shorter events, 1.4 us)
Async XLA Ops:
  0.0 1.0 copy-start
  0.0 7.1 %copy-start.6 = (bf16[64,2,1152]{2,1,0:T(2,128)(2,1)S(1)}, bf16[64,2,1152]{2,1,0:T(2,128)(2,1)}, u32[]{:S(2)}) copy-start(bf16[64,2,1152]{2,1,0:T(2,128)(2,1)} %param.11) | copy-start | bytes 884740
  0.0 7.2 %copy-start.7 = (s32[2]{0:T(128)S(1)}, s32[2]{0:T(128)}, u32[]{:S(2)}) copy-start(s32[2]{0:T(128)} %param.10) | copy-start | bytes 28
  7.8 0.8 copy-start.2
  7.8 1.2 copy-start.1
  9.2 1.1 slice-start
  10.2 2.0 %copy-start.3 = (bf16[1,288,1152]{2,1,0:T(8,128)(2,1)S(1)}, bf16[1,288,1152]{2,1,0:T(8,128)(2,1)}, u32[]{:S(2)}) copy-start(bf16[1,288,1152]{2,1,0:T(8,128)(2,1)} %param.16) | copy-start | bytes 1990660
  10.2 2.0 %copy-start.4 = (bf16[1,1152,288]{1,2,0:T(8,128)(2,1)S(1)}, bf16[1,1152,288]{1,2,0:T(8,128)(2,1)}, u32[]{:S(2)}) copy-start(bf16[1,1152,288]{1,2,0:T(8,128)(2,1)} %param.15) | copy-start | bytes 1990660
  10.2 2.0 %copy-start.5 = (bf16[1,1152,288]{1,2,0:T(8,128)(2,1)S(1)}, bf16[1,1152,288]{1,2,0:T(8,128)(2,1)}, u32[]{:S(2)}) copy-start(bf16[1,1152,288]{1,2,0:T(8,128)(2,1)} %param.14) | copy-start | bytes 1990660

commit v3 on v2

v3 whole, which is shorter than its diff:
```python
import functools

import jax
import jax.numpy as jnp
from jax import lax
from jax.experimental import pallas as pl
from jax.experimental.pallas import tpu as pltpu
from jax.sharding import PartitionSpec as P

MESH = pl.DeviceIdType.MESH
NT = (((1,), (1,)), ((), ()))
NN = (((1,), (0,)), ((), ()))
SIDE = 4
TILE = 16


EPS = 1e-06


def z_offsets(nz):
    order = [0]
    for step in range(1, nz):
        for way in (step, nz - step):
            if way not in order:
                order.append(way)
    return order


def cuts_of(chunks):
    half = (chunks + 1) // 2
    ends = (0, (half + 1) // 2, half, half + (chunks - half + 1) // 2, chunks)
    return [(ends[p], ends[p + 1]) for p in range(4)]


def expert_kernel(
    nz,
    w_ref,
    levels_ref,
    tok_ref,
    cot_ref,
    mod_ref,
    plan_ref,
    out_ref,
    wbuf,
    tbuf,
    xm,
    xe,
    ebuf,
    member,
    acc,
    pbuf,
    relay,
    in_r,
    in_l,
    fbuf,
    febuf,
    om,
    oe,
    w_loc,
    w_send,
    w_recv,
    wf_send,
    wf_recv,
    d_send,
    d_recv,
    e_send,
    e_recv,
    t_send,
    t_recv,
    tf_send,
    tf_recv,
    r_send,
    r_recv,
    o_send,
    o_recv,
    oe_send,
    oe_recv,
):
    n_exp = 2 * nz
    chunks = n_exp + 1
    width = w_ref.shape[-1]
    half = w_ref.shape[2]
    hidden = SIDE * 2 * half
    main = n_exp * TILE
    row_count = tok_ref.shape[0]
    images = levels_ref.shape[0]
    per_image = row_count // images
    f32, bf16 = jnp.float32, jnp.bfloat16

    s = lax.axis_index("seq")
    e = lax.axis_index("exp")
    core = lax.rem(e, 2)
    z = lax.div(e, 2)
    hi = lax.div(s, SIDE)
    lo = lax.rem(s, SIDE)
    w_at = (1 - core) * hi + core * lo
    t_at = (1 - core) * lo + core * hi
    w_step = SIDE - (SIDE - 1) * core
    t_step = 1 + (SIDE - 1) * core

    def on_w(offset):
        return (lax.rem(w_at + offset, SIDE) * w_step + t_at * t_step, e)

    def on_t(offset):
        return (w_at * w_step + lax.rem(t_at + offset, SIDE) * t_step, e)

    w_right, w_left = on_w(1), on_w(SIDE - 1)
    t_right, t_left = on_t(1), on_t(SIDE - 1)

    offsets = [(dz, dc) for dz in z_offsets(nz) for dc in (0, 1)]

    def peer(k, sign):
        dz, dc = offsets[k]
        if sign < 0:
            dz = (nz - dz) % nz
        return lax.rem(z + dz, nz) * 2 + lax.rem(core + dc, 2)

    def remote(src, dst, send, recv, device):
        return pltpu.make_async_remote_copy(
            src_ref=src,
            dst_ref=dst,
            send_sem=send,
            recv_sem=recv,
            device_id=device,
            device_id_type=MESH,
        )

    barrier = pltpu.get_barrier_semaphore()
    greeted = [w_right, w_left, t_right, t_left] + [(s, peer(k, 1)) for k in range(1, n_exp)]
    for device in greeted:
        pl.semaphore_signal(barrier, inc=1, device_id=device, device_id_type=MESH)
    pl.semaphore_wait(barrier, len(greeted))

    pieces = [(m, h) for m in range(3) for h in range(2)]
    w_right_copy = {}
    w_left_copy = {}
    for m, h in pieces:
        n = 2 * m + h
        w_right_copy[m, h] = remote(
            w_ref.at[m, h], wbuf.at[m, 1, h], w_send.at[0, n], w_recv.at[0, n], w_right
        )
        w_left_copy[m, h] = remote(
            w_ref.at[m, h], wbuf.at[m, 2, h], w_send.at[1, n], w_recv.at[1, n], w_left
        )
    for m in range(3):
        w_right_copy[m, 0].start()
        w_left_copy[m, 1].start()
    for m in range(3):
        w_right_copy[m, 1].start()
        w_left_copy[m, 0].start()
    w_local = [
        pltpu.make_async_copy(w_ref.at[m, h], wbuf.at[m, 0, h], w_loc.at[2 * m + h])
        for m, h in pieces
    ]
    for copy in w_local:
        copy.start()

    def scale_shift(i):
        row = mod_ref[levels_ref[i]].astype(f32)
        return 1.0 + row[0:1, :], row[1:2, :]

    def root(x):
        return jnp.sqrt(jnp.mean(x * x, axis=-1, keepdims=True) + EPS)

    normed = []
    for i in range(images):
        x = tok_ref[i * per_image : (i + 1) * per_image, :].astype(f32)
        gain, shift = scale_shift(i)
        normed.append((x / root(x) * gain + shift).astype(bf16))
    normed = jnp.concatenate(normed, axis=0)
    plan = plan_ref[...]
    route = [plan[0:1, :], plan[1:2, :]]
    code = [plan[2:3, :].astype(f32), plan[3:4, :].astype(f32)]
    code_sum = code[0] + code[1]
    expert = lax.broadcasted_iota(jnp.int32, (n_exp, row_count), 0)
    hit = [jnp.where(route[r] == expert, 1.0, 0.0) for r in range(2)]
    hits = hit[0] + hit[1]
    gates = hit[0] * (code[0] / code_sum) + hit[1] * (code[1] / code_sum)
    before = lax.broadcasted_iota(jnp.int32, (row_count, row_count), 0)
    after = lax.broadcasted_iota(jnp.int32, (row_count, row_count), 1)
    prior = jnp.where(before < after, 1.0, 0.0).astype(bf16)
    place = lax.dot_general(hits.astype(bf16), prior, NN, preferred_element_type=f32)
    slot = lax.broadcasted_iota(jnp.int32, (main, n_exp), 0)
    owner = lax.broadcasted_iota(jnp.int32, (main, n_exp), 1)
    spread = jnp.where(lax.div(slot, TILE) == owner, 1.0, 0.0)
    spread16 = spread.astype(bf16)
    hits_at = lax.dot_general(spread16, hits.astype(bf16), NN, preferred_element_type=f32)
    place_at = lax.dot_general(spread16, place.astype(bf16), NN, preferred_element_type=f32)
    gates_at = lax.dot_general(
        spread, gates, NN, preferred_element_type=f32, precision=lax.Precision.HIGHEST
    )
    wanted = lax.rem(lax.broadcasted_iota(jnp.int32, (main, row_count), 0), TILE).astype(f32)
    pick = jnp.where(place_at == wanted, hits_at, 0.0)
    pick_last = jnp.where(place == float(TILE), hits, 0.0)
    gate_of = jnp.sum(pick * gates_at, axis=1, keepdims=True)
    gate_of_last = jnp.sum(pick_last * gates, axis=1, keepdims=True)
    member[0:main, :] = pick.astype(bf16)
    member[main:, :] = pick_last.astype(bf16)
    rows = lax.dot_general(member[...], normed, NN, preferred_element_type=f32)
    grads = lax.dot_general(member[...], cot_ref[...], NN, preferred_element_type=f32)
    xm[:, 0:TILE, :] = rows[0:main].astype(bf16).reshape(n_exp, TILE, width)
    xm[:, TILE : 2 * TILE, :] = (grads[0:main] * gate_of).astype(bf16).reshape(n_exp, TILE, width)
    xe[:, 0, :] = rows[main:]
    xe[:, 1, :] = (grads[main:] * gate_of_last).astype(bf16).astype(f32)

    d_copy = [pltpu.make_async_copy(xm.at[e], tbuf.at[0, 0], d_recv.at[0])]
    e_copy = [pltpu.make_async_copy(xe.at[e], ebuf.at[0], e_recv.at[0])]
    for k in range(1, n_exp):
        there = peer(k, 1)
        d_copy.append(
            remote(xm.at[there], tbuf.at[0, k], d_send.at[k], d_recv.at[k], (s, there))
        )
        e_copy.append(remote(xe.at[there], ebuf.at[k], e_send.at[k], e_recv.at[k], (s, there)))
    for k in range(n_exp):
        d_copy[k].start()
        e_copy[k].start()

    wf_right = [
        remote(wbuf.at[m, 1, 0], wbuf.at[m, 3, 0], wf_send.at[0, m], wf_recv.at[0, m], w_right)
        for m in range(3)
    ]
    wf_left = [
        remote(wbuf.at[m, 2, 1], wbuf.at[m, 3, 1], wf_send.at[1, m], wf_recv.at[1, m], w_left)
        for m in range(3)
    ]
    for m in range(3):
        w_right_copy[m, 0].wait_recv()
        wf_right[m].start()
        w_left_copy[m, 1].wait_recv()
        wf_left[m].start()

    cuts = cuts_of(chunks)

    def part(p):
        return pl.ds(cuts[p][0], cuts[p][1] - cuts[p][0])

    tr_copy = [
        remote(tbuf.at[0, part(p)], tbuf.at[1, part(p)], t_send.at[0, p], t_recv.at[0, p], t_right)
        for p in range(4)
    ]
    tl_copy = [
        remote(tbuf.at[0, part(p)], tbuf.at[2, part(p)], t_send.at[1, p], t_recv.at[1, p], t_left)
        for p in range(4)
    ]
    tf_copy = [
        remote(
            tbuf.at[1 + p % 2, part(p)],
            tbuf.at[3, part(p)],
            tf_send.at[p],
            tf_recv.at[p],
            t_left if p % 2 else t_right,
        )
        for p in range(4)
    ]

    def weights_phase_one():
        for m in range(3):
            w_right_copy[m, 1].wait_recv()
            w_left_copy[m, 0].wait_recv()

    def weights_phase_two():
        for m in range(3):
            wf_right[m].wait_recv()
            wf_left[m].wait_recv()

    weights_phase_one()
    for p in range(4):
        for k in range(*cuts[p]):
            if k == 0:
                d_copy[k].wait()
            elif k < n_exp:
                d_copy[k].wait_recv()
            else:
                e_copy[0].wait()
                for j in range(1, n_exp):
                    e_copy[j].wait_recv()
                tbuf[0, n_exp, 0:TILE, :] = ebuf[:, 0, :].astype(bf16)
                tbuf[0, n_exp, TILE : 2 * TILE, :] = ebuf[:, 1, :].astype(bf16)
        tr_copy[p].start()
        tl_copy[p].start()
    for copy in w_local:
        copy.wait()
    weights_phase_two()

    def pass_on(p):
        tr_copy[p].wait_recv()
        tl_copy[p].wait_recv()
        tf_copy[p].start()

    def compute(slots, first, last):
        count = (last - first) * TILE

        def taken(lower):
            found = [
                tbuf[i, first:last, lower : lower + TILE, :].reshape(count, width) for i in slots
            ]
            return found[0] if len(found) == 1 else jnp.concatenate(found, axis=0)

        rows_in, grads_in = taken(0), taken(TILE)
        gate = wbuf[0].reshape(hidden, width)
        up = wbuf[1].reshape(hidden, width)
        down = wbuf[2].reshape(hidden, width)
        gate_pre = lax.dot_general(rows_in, gate, NT, preferred_element_type=f32)
        up_pre = lax.dot_general(rows_in, up, NT, preferred_element_type=f32)
        grad_hidden = lax.dot_general(grads_in, down, NT, preferred_element_type=f32)
        sigma = 1.0 / (1.0 + jnp.exp(-gate_pre))
        scaled = grad_hidden * sigma
        grad_gate = (scaled * up_pre * (1.0 + gate_pre * (1.0 - sigma))).astype(bf16)
        grad_up = (scaled * gate_pre).astype(bf16)
        back = lax.dot_general(grad_gate, gate, NN, preferred_element_type=f32)
        back += lax.dot_general(grad_up, up, NN, preferred_element_type=f32)
        for n, i in enumerate(slots):
            acc[i, first * TILE : last * TILE, :] = back[n * count : (n + 1) * count]

    def span(p):
        return cuts[p][0] * TILE, cuts[p][1] * TILE

    def ds_of(p):
        lower, upper = span(p)
        return pl.ds(lower, upper - lower)

    o_part, l_part, r_part = [], [], []
    for p in range(4):
        rows_p = ds_of(p)
        o_part.append(
            remote(
                pbuf.at[0, rows_p],
                relay.at[rows_p],
                r_send.at[0, p],
                r_recv.at[0, p],
                t_right if p % 2 else t_left,
            )
        )
        l_part.append(
            remote(pbuf.at[1, rows_p], in_r.at[rows_p], r_send.at[1, p], r_recv.at[1, p], t_left)
        )
        r_part.append(
            remote(pbuf.at[2, rows_p], in_l.at[rows_p], r_send.at[2, p], r_recv.at[2, p], t_right)
        )

    def send_plain(n, i, p, copy):
        lower, upper = span(p)
        pbuf[n, lower:upper, :] = acc[i, lower:upper, :].astype(bf16)
        copy.start()

    def send_added(n, i, p, copy):
        lower, upper = span(p)
        o_part[p].wait_recv()
        added = acc[i, lower:upper, :] + relay[lower:upper, :].astype(f32)
        pbuf[n, lower:upper, :] = added.astype(bf16)
        copy.start()

    mine = pltpu.make_async_copy(fbuf.at[0], om.at[e], o_recv.at[0])
    mine_e = pltpu.make_async_copy(febuf.at[0], oe.at[e], oe_recv.at[0])
    o_copy, oe_copy = [mine], [mine_e]
    for k in range(1, n_exp):
        there = peer(k, -1)
        o_copy.append(remote(fbuf.at[k], om.at[e], o_send.at[k], o_recv.at[k], (s, there)))
        oe_copy.append(remote(febuf.at[k], oe.at[e], oe_send.at[k], oe_recv.at[k], (s, there)))

    def finish(first, last, parts):
        for p in parts:
            l_part[p].wait_recv()
            r_part[p].wait_recv()
        lower, upper = first * TILE, last * TILE
        total = acc[0, lower:upper, :] + in_r[lower:upper, :].astype(f32)
        total = (total + in_l[lower:upper, :].astype(f32)).astype(bf16)
        fbuf[first:last] = total.reshape(last - first, TILE, width)
        for k in range(first, min(last, n_exp)):
            o_copy[k].start()
        if last > n_exp:
            febuf[:, 0, :] = total[(n_exp - first) * TILE :, :].astype(f32)
            for k in range(n_exp):
                oe_copy[k].start()

    middle = cuts[2][0]
    compute((0,), 0, chunks)
    pass_on(0)
    pass_on(1)
    compute((1, 2), 0, middle)
    send_plain(1, 1, 1, l_part[1])
    send_plain(2, 2, 0, r_part[0])
    pass_on(2)
    pass_on(3)
    tf_copy[0].wait_recv()
    tf_copy[1].wait_recv()
    compute((3,), 0, middle)
    send_plain(0, 3, 0, o_part[0])
    send_plain(0, 3, 1, o_part[1])
    tf_copy[2].wait_recv()
    tf_copy[3].wait_recv()
    compute((3,), middle, chunks)
    send_plain(0, 3, 2, o_part[2])
    send_plain(0, 3, 3, o_part[3])
    send_added(1, 1, 0, l_part[0])
    send_added(2, 2, 1, r_part[1])
    compute((1, 2), middle, chunks)
    send_plain(1, 1, 3, l_part[3])
    send_plain(2, 2, 2, r_part[2])
    send_added(1, 1, 2, l_part[2])
    send_added(2, 2, 3, r_part[3])
    finish(0, middle, (0, 1))
    finish(middle, chunks, (2, 3))

    for group in (
        w_right_copy.values(),
        w_left_copy.values(),
        wf_right,
        wf_left,
        d_copy[1:],
        e_copy[1:],
        tr_copy,
        tl_copy,
        tf_copy,
        o_part,
        l_part,
        r_part,
    ):
        for copy in group:
            copy.wait_send()
    mine.wait()
    mine_e.wait()
    for k in range(1, n_exp):
        here = peer(k, 1)
        o_copy[k].wait_send()
        oe_copy[k].wait_send()
        remote(fbuf.at[k], om.at[here], o_send.at[k], o_recv.at[k], (s, here)).wait_recv()
        remote(febuf.at[k], oe.at[here], oe_send.at[k], oe_recv.at[k], (s, here)).wait_recv()

    om[n_exp] = oe[:, 0, :].astype(bf16)
    grad_normed = lax.dot_general(
        member[...],
        om[...].reshape(chunks * TILE, width),
        (((0,), (0,)), ((), ())),
        preferred_element_type=f32,
    )
    for i in range(images):
        lower, upper = i * per_image, (i + 1) * per_image
        x = tok_ref[lower:upper, :].astype(f32)
        gain, shift = scale_shift(i)
        inverse = 1.0 / root(x)
        g = grad_normed[lower:upper, :] * gain
        y = x * inverse
        out = inverse * (g - y * jnp.mean(g * y, axis=-1, keepdims=True))
        out_ref[lower:upper, :] = out.astype(bf16)


def run_experts(weights, levels, tokens, cotangent, modulation, plan, n_exp):
    row_count, width = tokens.shape
    half = weights.shape[2]
    chunks = n_exp + 1
    rows_count = chunks * TILE
    bf16, f32 = jnp.bfloat16, jnp.float32
    dma = pltpu.SemaphoreType.DMA
    vmem = pl.BlockSpec(memory_space=pltpu.VMEM)
    return pl.pallas_call(
        functools.partial(expert_kernel, n_exp // 2),
        out_shape=jax.ShapeDtypeStruct((row_count, width), bf16),
        in_specs=[
            pl.BlockSpec(memory_space=pl.ANY),
            pl.BlockSpec(memory_space=pltpu.SMEM),
            vmem,
            vmem,
            vmem,
            vmem,
        ],
        out_specs=vmem,
        scratch_shapes=[
            pltpu.VMEM((3, SIDE, 2, half, width), bf16),
            pltpu.VMEM((SIDE, chunks, 2 * TILE, width), bf16),
            pltpu.VMEM((n_exp, 2 * TILE, width), bf16),
            pltpu.VMEM((n_exp, 2, width), f32),
            pltpu.VMEM((n_exp, 2, width), f32),
            pltpu.VMEM((rows_count, row_count), bf16),
            pltpu.VMEM((SIDE, rows_count, width), f32),
            pltpu.VMEM((3, rows_count, width), bf16),
            pltpu.VMEM((rows_count, width), bf16),
            pltpu.VMEM((rows_count, width), bf16),
            pltpu.VMEM((rows_count, width), bf16),
            pltpu.VMEM((chunks, TILE, width), bf16),
            pltpu.VMEM((n_exp, 1, width), f32),
            pltpu.VMEM((chunks, TILE, width), bf16),
            pltpu.VMEM((n_exp, 1, width), f32),
            dma((6,)),
            dma((2, 6)),
            dma((2, 6)),
            dma((2, 3)),
            dma((2, 3)),
            dma((n_exp,)),
            dma((n_exp,)),
            dma((n_exp,)),
            dma((n_exp,)),
            dma((2, 4)),
            dma((2, 4)),
            dma((4,)),
            dma((4,)),
            dma((3, 4)),
            dma((3, 4)),
            dma((n_exp,)),
            dma((n_exp,)),
            dma((n_exp,)),
            dma((n_exp,)),
        ],
        compiler_params=pltpu.CompilerParams(
            collective_id=0, has_side_effects=True, vmem_limit_bytes=60 * 2**20
        ),
        name="experts",
    )(weights, levels, tokens, cotangent, modulation, plan)


def per_device(
    tokens,
    timesteps,
    modulation,
    routes,
    gate_codes,
    gate_weight,
    up_weight,
    down_weight,
    cotangent,
):
    img_local, patch_local, width = tokens.shape
    top_count = routes.shape[3]
    row_count = img_local * patch_local
    block_width = gate_weight.shape[2]
    plan = jnp.concatenate(
        [
            jnp.transpose(routes[0], (2, 1, 0)).reshape(top_count, row_count),
            jnp.transpose(gate_codes, (2, 0, 1)).reshape(top_count, row_count),
        ]
    )
    weights = jnp.stack(
        [jnp.swapaxes(gate_weight[0], 0, 1), jnp.swapaxes(up_weight[0], 0, 1), down_weight[0]]
    ).reshape(3, 2, block_width // 2, width)
    grad_tokens = run_experts(
        weights,
        timesteps,
        tokens.reshape(row_count, width),
        cotangent.reshape(row_count, width),
        modulation,
        plan,
        lax.axis_size("exp"),
    )
    return grad_tokens.reshape(img_local, patch_local, width)


def solution(mesh):
    in_specs = (
        P("exp", "seq", None),
        P("exp"),
        P(),
        P("exp", "seq", None, None),
        P("exp", "seq", None),
        P("exp", None, "seq"),
        P("exp", None, "seq"),
        P("exp", "seq", None),
        P("exp", "seq", None),
    )
    out_specs = P("exp", "seq", None)
    return jax.shard_map(
        per_device, mesh=mesh, in_specs=in_specs, out_specs=out_specs, check_vma=False
    )
```

time: 128 us -> 109 us (0.85)
  Pallas kernels: 110 us -> 102 us
  other arithmetic: 9.67 us -> 3.62 us
  matrix products: 2.44 us -> 0 us
  local copies, waits for them, and re-layouts: 4.94 us -> 3.23 us
    pallas_call x1, Pallas kernels: 110 us -> 102 us  [run_experts(): pl.pallas_call(functools.partial(expert_kernel, n_exp // 2), out_shape=ja...]
    convert_element_type x6 -> x0, other arithmetic: 3.57 us -> none  [the longest x1 0.94 us: per_device(): back_extra.reshape(n_exp, feature_width).astype(jnp.bfloat16)]
    dot_general x4 -> x0, matrix products: 2.44 us -> none  [the longest x1 1.55 us: per_device(): jnp.dot(member, slot_backs, preferred_element_type=jnp.float32)]
    reduce_sum x4 -> x0, other arithmetic: 2.06 us -> none  [the longest x1 1.1 us: normalize_modulate(): mean_square = jnp.mean(tokens_f * tokens_f, axis=-1, keepdims=True)]
    another operation x1, other arithmetic: 1.54 us -> 3.03 us  [per_device(): jnp.stack([jnp.swapaxes(gate_weight[0], 0, 1), jnp.swapaxes(up_weight[0],...]
where the time goes in v3:
time: 109 us
  Pallas kernels  102 us (94%)
  other arithmetic  3.62 us (3%)
  local copies, waits for them, and re-layouts  3.23 us (3%)
    pallas_call x1, Pallas kernels, run_experts(): pl.pallas_call(functools.partial(expert_kernel, n_exp // 2), out_shape=ja...  102 us
    another operation x1, other arithmetic, per_device(): jnp.stack([jnp.swapaxes(gate_weight[0], 0, 1), jnp.swapaxes(up_weight[0],...  3.03 us

profile of v3, /device:TPU:1, one launch (start us, length us, event | category | flops | bytes accessed | tf_op | source)
XLA Modules:
  0.0 109.0 jit_solution(4293564075549249791)
XLA Ops:
  0.0 0.7 copy.10
  0.7 0.1 reshape.23
  0.8 0.7 copy.11
  1.5 0.1 reshape.24
  1.5 0.6 pad_add_fusion.plan_ref
  2.1 3.0 %pad_maximum_fusion.w_ref = bf16[3,2,144,1152]{3,2,1,0:T(8,128)(2,1)} fusion(bf16[1,2,144,1152]{3,2,1,0:T(8,128)(2,1)} %bitcast.19, bf16[1,2,144,1152]{3,2,1,0:T(8,128)(2,1)} %bitcast.20, bf16[1,2,144,1152]{3,2,1,0:T(8,128)(2,1)} %bitcast.21), kind=kLoop, calls=%fused_computation | loop fusion | flops 1990656 | bytes 3981312 | tf_op jit(solution)/shard_map/stack | solution.py:532
  5.2 102.2 %experts.1 = bf16[128,1152]{1,0:T(8,128)(2,1)} custom-call(bf16[3,2,144,1152]{3,2,1,0:T(8,128)(2,1)} %pad_maximum_fusion.w_ref, s32[2]{0:T(128)} %levels_ref.1, bf16[128,1152]{1,0:T(8,128)(2,1)} %bitcast.22, bf16[128,1152]{1,0:T(8,128)(2,1)} %bitcast.23, bf16[64,2,1152]{2,1,0:T(2,128)(2,1)} %mod_ref.1, s32[4,128]{1,0:T(4,128)} %pad_add_fusion.plan_ref), custom_call_target="tpu_custom_call" | custom-call | tf_op jit(solution)/shard_map/experts/pallas_call | solution.py:456
  107.3 1.7 %copy.13 = bf16[2,64,1152]{2,1,0:T(8,128)(2,1)} copy(bf16[2,64,1152]{2,1,0:T(8,128)(2,1)} %bitcast.18) | data formatting | bytes 589824

commit v4 on v3

--- a/solution.py
+++ b/solution.py
@@ -27,19 +27,22 @@
 
 
 def cuts_of(chunks):
-    half = (chunks + 1) // 2
-    ends = (0, (half + 1) // 2, half, half + (chunks - half + 1) // 2, chunks)
+    first = (chunks + 1) // 2
+    ends = (0, (first + 1) // 2, first, first + (chunks - first + 1) // 2, chunks)
     return [(ends[p], ends[p + 1]) for p in range(4)]
 
 
 def expert_kernel(
     nz,
-    w_ref,
+    gate_ref,
+    up_ref,
+    down_ref,
     levels_ref,
     tok_ref,
     cot_ref,
     mod_ref,
-    plan_ref,
+    route_ref,
+    code_ref,
     out_ref,
     wbuf,
     tbuf,
@@ -78,8 +81,8 @@
 ):
     n_exp = 2 * nz
     chunks = n_exp + 1
-    width = w_ref.shape[-1]
-    half = w_ref.shape[2]
+    w_refs = (gate_ref, up_ref, down_ref)
+    _, half, width = gate_ref.shape
     hidden = SIDE * 2 * half
     main = n_exp * TILE
     row_count = tok_ref.shape[0]
@@ -107,7 +110,8 @@
     w_right, w_left = on_w(1), on_w(SIDE - 1)
     t_right, t_left = on_t(1), on_t(SIDE - 1)
 
-    offsets = [(dz, dc) for dz in z_offsets(nz) for dc in (0, 1)]
+    offsets = [(dz, dc) for dz in reversed(z_offsets(nz)) for dc in (1, 0)]
+    here = n_exp - 1
 
     def peer(k, sign):
         dz, dc = offsets[k]
@@ -126,21 +130,27 @@
         )
 
     barrier = pltpu.get_barrier_semaphore()
-    greeted = [w_right, w_left, t_right, t_left] + [(s, peer(k, 1)) for k in range(1, n_exp)]
+    greeted = [w_right, w_left, t_right, t_left] + [(s, peer(k, 1)) for k in range(here)]
     for device in greeted:
         pl.semaphore_signal(barrier, inc=1, device_id=device, device_id_type=MESH)
+    pieces = [(m, h) for m in range(3) for h in range(2)]
+    w_local = [
+        pltpu.make_async_copy(w_refs[m].at[h], wbuf.at[m, 0, h], w_loc.at[2 * m + h])
+        for m, h in pieces
+    ]
+    for copy in w_local:
+        copy.start()
     pl.semaphore_wait(barrier, len(greeted))
 
-    pieces = [(m, h) for m in range(3) for h in range(2)]
     w_right_copy = {}
     w_left_copy = {}
     for m, h in pieces:
         n = 2 * m + h
         w_right_copy[m, h] = remote(
-            w_ref.at[m, h], wbuf.at[m, 1, h], w_send.at[0, n], w_recv.at[0, n], w_right
+            w_refs[m].at[h], wbuf.at[m, 1, h], w_send.at[0, n], w_recv.at[0, n], w_right
         )
         w_left_copy[m, h] = remote(
-            w_ref.at[m, h], wbuf.at[m, 2, h], w_send.at[1, n], w_recv.at[1, n], w_left
+            w_refs[m].at[h], wbuf.at[m, 2, h], w_send.at[1, n], w_recv.at[1, n], w_left
         )
     for m in range(3):
         w_right_copy[m, 0].start()
@@ -148,12 +158,6 @@
     for m in range(3):
         w_right_copy[m, 1].start()
         w_left_copy[m, 0].start()
-    w_local = [
-        pltpu.make_async_copy(w_ref.at[m, h], wbuf.at[m, 0, h], w_loc.at[2 * m + h])
-        for m, h in pieces
-    ]
-    for copy in w_local:
-        copy.start()
 
     def scale_shift(i):
         row = mod_ref[levels_ref[i]].astype(f32)
@@ -168,11 +172,20 @@
         gain, shift = scale_shift(i)
         normed.append((x / root(x) * gain + shift).astype(bf16))
     normed = jnp.concatenate(normed, axis=0)
-    plan = plan_ref[...]
-    route = [plan[0:1, :], plan[1:2, :]]
-    code = [plan[2:3, :].astype(f32), plan[3:4, :].astype(f32)]
+    image_row = lax.broadcasted_iota(jnp.int32, (per_image, row_count), 0)
+    any_row = lax.broadcasted_iota(jnp.int32, (per_image, row_count), 1)
+
+    def laid_out(ref):
+        found = jnp.zeros((2, row_count), f32)
+        for i in range(images):
+            lay = jnp.where(any_row - i * per_image == image_row, 1.0, 0.0).astype(bf16)
+            values = ref[i].astype(f32).astype(bf16)
+            found += lax.dot_general(values, lay, NN, preferred_element_type=f32)
+        return [found[0:1, :], found[1:2, :]]
+
+    route, code = laid_out(route_ref), laid_out(code_ref)
     code_sum = code[0] + code[1]
-    expert = lax.broadcasted_iota(jnp.int32, (n_exp, row_count), 0)
+    expert = lax.broadcasted_iota(jnp.int32, (n_exp, row_count), 0).astype(f32)
     hit = [jnp.where(route[r] == expert, 1.0, 0.0) for r in range(2)]
     hits = hit[0] + hit[1]
     gates = hit[0] * (code[0] / code_sum) + hit[1] * (code[1] / code_sum)
@@ -203,14 +216,15 @@
     xe[:, 0, :] = rows[main:]
     xe[:, 1, :] = (grads[main:] * gate_of_last).astype(bf16).astype(f32)
 
-    d_copy = [pltpu.make_async_copy(xm.at[e], tbuf.at[0, 0], d_recv.at[0])]
-    e_copy = [pltpu.make_async_copy(xe.at[e], ebuf.at[0], e_recv.at[0])]
-    for k in range(1, n_exp):
+    d_copy, e_copy = [], []
+    for k in range(here):
         there = peer(k, 1)
         d_copy.append(
-            remote(xm.at[there], tbuf.at[0, k], d_send.at[k], d_recv.at[k], (s, there))
+            remote(xm.at[there], tbuf.at[0, k + 1], d_send.at[k], d_recv.at[k], (s, there))
         )
         e_copy.append(remote(xe.at[there], ebuf.at[k], e_send.at[k], e_recv.at[k], (s, there)))
+    d_copy.append(pltpu.make_async_copy(xm.at[e], tbuf.at[0, here + 1], d_recv.at[here]))
+    e_copy.append(pltpu.make_async_copy(xe.at[e], ebuf.at[here], e_recv.at[here]))
     for k in range(n_exp):
         d_copy[k].start()
         e_copy[k].start()
@@ -258,34 +272,42 @@
             w_right_copy[m, 1].wait_recv()
             w_left_copy[m, 0].wait_recv()
 
-    def weights_phase_two():
-        for m in range(3):
+    def weights_phase_two(first, last):
+        for m in range(first, last):
             wf_right[m].wait_recv()
             wf_left[m].wait_recv()
 
-    weights_phase_one()
-    for p in range(4):
-        for k in range(*cuts[p]):
-            if k == 0:
-                d_copy[k].wait()
-            elif k < n_exp:
-                d_copy[k].wait_recv()
+    def arrive(p):
+        for c in range(*cuts[p]):
+            if c == 0:
+                for k in range(here):
+                    e_copy[k].wait_recv()
+                e_copy[here].wait()
+                tbuf[0, 0, 0:TILE, :] = ebuf[:, 0, :].astype(bf16)
+                tbuf[0, 0, TILE : 2 * TILE, :] = ebuf[:, 1, :].astype(bf16)
+            elif c == here + 1:
+                d_copy[here].wait()
             else:
-                e_copy[0].wait()
-                for j in range(1, n_exp):
-                    e_copy[j].wait_recv()
-                tbuf[0, n_exp, 0:TILE, :] = ebuf[:, 0, :].astype(bf16)
-                tbuf[0, n_exp, TILE : 2 * TILE, :] = ebuf[:, 1, :].astype(bf16)
+                d_copy[c - 1].wait_recv()
+
+    def send_rows(p):
         tr_copy[p].start()
         tl_copy[p].start()
-    for copy in w_local:
-        copy.wait()
-    weights_phase_two()
 
     def pass_on(p):
         tr_copy[p].wait_recv()
         tl_copy[p].wait_recv()
         tf_copy[p].start()
+
+    for p in range(4):
+        arrive(p)
+    weights_phase_one()
+    weights_phase_two(0, 1)
+    send_rows(0)
+    send_rows(1)
+    for copy in w_local:
+        copy.wait()
+    weights_phase_two(1, 3)
 
     def compute(slots, first, last):
         count = (last - first) * TILE
@@ -350,13 +372,15 @@
         pbuf[n, lower:upper, :] = added.astype(bf16)
         copy.start()
 
-    mine = pltpu.make_async_copy(fbuf.at[0], om.at[e], o_recv.at[0])
-    mine_e = pltpu.make_async_copy(febuf.at[0], oe.at[e], oe_recv.at[0])
-    o_copy, oe_copy = [mine], [mine_e]
-    for k in range(1, n_exp):
+    o_copy, oe_copy = [], []
+    for k in range(here):
         there = peer(k, -1)
-        o_copy.append(remote(fbuf.at[k], om.at[e], o_send.at[k], o_recv.at[k], (s, there)))
+        o_copy.append(remote(fbuf.at[k + 1], om.at[e], o_send.at[k], o_recv.at[k], (s, there)))
         oe_copy.append(remote(febuf.at[k], oe.at[e], oe_send.at[k], oe_recv.at[k], (s, there)))
+    mine = pltpu.make_async_copy(fbuf.at[here + 1], om.at[e], o_recv.at[here])
+    mine_e = pltpu.make_async_copy(febuf.at[here], oe.at[e], oe_recv.at[here])
+    o_copy.append(mine)
+    oe_copy.append(mine_e)
 
     def finish(first, last, parts):
         for p in parts:
@@ -366,10 +390,10 @@
         total = acc[0, lower:upper, :] + in_r[lower:upper, :].astype(f32)
         total = (total + in_l[lower:upper, :].astype(f32)).astype(bf16)
         fbuf[first:last] = total.reshape(last - first, TILE, width)
-        for k in range(first, min(last, n_exp)):
-            o_copy[k].start()
-        if last > n_exp:
-            febuf[:, 0, :] = total[(n_exp - first) * TILE :, :].astype(f32)
+        for c in range(max(first, 1), last):
+            o_copy[c - 1].start()
+        if first == 0:
+            febuf[:, 0, :] = total[0:TILE, :].astype(f32)
             for k in range(n_exp):
                 oe_copy[k].start()
 
@@ -377,29 +401,31 @@
     compute((0,), 0, chunks)
     pass_on(0)
     pass_on(1)
+    send_rows(2)
+    send_rows(3)
     compute((1, 2), 0, middle)
     send_plain(1, 1, 1, l_part[1])
     send_plain(2, 2, 0, r_part[0])
-    pass_on(2)
-    pass_on(3)
     tf_copy[0].wait_recv()
     tf_copy[1].wait_recv()
     compute((3,), 0, middle)
     send_plain(0, 3, 0, o_part[0])
     send_plain(0, 3, 1, o_part[1])
+    pass_on(2)
+    pass_on(3)
+    compute((1, 2), middle, chunks)
+    send_plain(1, 1, 3, l_part[3])
+    send_plain(2, 2, 2, r_part[2])
+    send_added(1, 1, 0, l_part[0])
+    send_added(2, 2, 1, r_part[1])
     tf_copy[2].wait_recv()
     tf_copy[3].wait_recv()
     compute((3,), middle, chunks)
     send_plain(0, 3, 2, o_part[2])
     send_plain(0, 3, 3, o_part[3])
-    send_added(1, 1, 0, l_part[0])
-    send_added(2, 2, 1, r_part[1])
-    compute((1, 2), middle, chunks)
-    send_plain(1, 1, 3, l_part[3])
-    send_plain(2, 2, 2, r_part[2])
+    finish(0, middle, (0, 1))
     send_added(1, 1, 2, l_part[2])
     send_added(2, 2, 3, r_part[3])
-    finish(0, middle, (0, 1))
     finish(middle, chunks, (2, 3))
 
     for group in (
@@ -407,8 +433,8 @@
         w_left_copy.values(),
         wf_right,
         wf_left,
-        d_copy[1:],
-        e_copy[1:],
+        d_copy[:here],
+        e_copy[:here],
         tr_copy,
         tl_copy,
         tf_copy,
@@ -420,12 +446,12 @@
             copy.wait_send()
     mine.wait()
     mine_e.wait()
-    for k in range(1, n_exp):
-        here = peer(k, 1)
+    for k in range(here):
+        whose = peer(k, 1)
         o_copy[k].wait_send()
         oe_copy[k].wait_send()
-        remote(fbuf.at[k], om.at[here], o_send.at[k], o_recv.at[k], (s, here)).wait_recv()
-        remote(febuf.at[k], oe.at[here], oe_send.at[k], oe_recv.at[k], (s, here)).wait_recv()
+        remote(fbuf.at[k + 1], om.at[whose], o_send.at[k], o_recv.at[k], (s, whose)).wait_recv()
+        remote(febuf.at[k], oe.at[whose], oe_send.at[k], oe_recv.at[k], (s, whose)).wait_recv()
 
     om[n_exp] = oe[:, 0, :].astype(bf16)
     grad_normed = lax.dot_general(
@@ -445,20 +471,24 @@
         out_ref[lower:upper, :] = out.astype(bf16)
 
 
-def run_experts(weights, levels, tokens, cotangent, modulation, plan, n_exp):
+def run_experts(weights, levels, tokens, cotangent, modulation, routes, codes, n_exp):
     row_count, width = tokens.shape
-    half = weights.shape[2]
+    half = weights[0].shape[1]
     chunks = n_exp + 1
     rows_count = chunks * TILE
     bf16, f32 = jnp.bfloat16, jnp.float32
     dma = pltpu.SemaphoreType.DMA
     vmem = pl.BlockSpec(memory_space=pltpu.VMEM)
+    anywhere = pl.BlockSpec(memory_space=pl.ANY)
     return pl.pallas_call(
         functools.partial(expert_kernel, n_exp // 2),
         out_shape=jax.ShapeDtypeStruct((row_count, width), bf16),
         in_specs=[
-            pl.BlockSpec(memory_space=pl.ANY),
+            anywhere,
+            anywhere,
+            anywhere,
             pl.BlockSpec(memory_space=pltpu.SMEM),
+            vmem,
             vmem,
             vmem,
             vmem,
@@ -505,7 +535,7 @@
             collective_id=0, has_side_effects=True, vmem_limit_bytes=60 * 2**20
         ),
         name="experts",
-    )(weights, levels, tokens, cotangent, modulation, plan)
+    )(*weights, levels, tokens, cotangent, modulation, routes, codes)
 
 
 def per_device(
@@ -520,25 +550,24 @@
     cotangent,
 ):
     img_local, patch_local, width = tokens.shape
-    top_count = routes.shape[3]
     row_count = img_local * patch_local
     block_width = gate_weight.shape[2]
-    plan = jnp.concatenate(
-        [
-            jnp.transpose(routes[0], (2, 1, 0)).reshape(top_count, row_count),
-            jnp.transpose(gate_codes, (2, 0, 1)).reshape(top_count, row_count),
-        ]
-    )
-    weights = jnp.stack(
-        [jnp.swapaxes(gate_weight[0], 0, 1), jnp.swapaxes(up_weight[0], 0, 1), down_weight[0]]
-    ).reshape(3, 2, block_width // 2, width)
+    weights = [
+        w.reshape(2, block_width // 2, width)
+        for w in (
+            jnp.swapaxes(gate_weight[0], 0, 1),
+            jnp.swapaxes(up_weight[0], 0, 1),
+            down_weight[0],
+        )
+    ]
     grad_tokens = run_experts(
         weights,
         timesteps,
         tokens.reshape(row_count, width),
         cotangent.reshape(row_count, width),
         modulation,
-        plan,
+        jnp.transpose(routes[0], (1, 2, 0)),
+        jnp.transpose(gate_codes, (0, 2, 1)),
         lax.axis_size("exp"),
     )
     return grad_tokens.reshape(img_local, patch_local, width)

time: 109 us -> 97.5 us (0.89)
  Pallas kernels: 102 us -> 95.7 us
  other arithmetic: 3.62 us -> 0 us
  local copies, waits for them, and re-layouts: 3.23 us -> 1.7 us
    pallas_call x1, Pallas kernels: 102 us -> 95.7 us  [run_experts(): pl.pallas_call(functools.partial(expert_kernel, n_exp // 2), out_shape=ja...]
    another operation x1 -> x0, other arithmetic: 3.03 us -> none  [per_device(): jnp.stack([jnp.swapaxes(gate_weight[0], 0, 1), jnp.swapaxes(up_weight[0],...]
    transpose x2 -> x0, local copies, waits for them, and re-layouts: 1.37 us -> none  [the longest x1 0.68 us: per_device(): jnp.transpose(gate_codes, (2, 0, 1)).reshape(top_count, row_count)]
where the time goes in v4:
time: 97.5 us; the launch traced here: 97.4 us
  Pallas kernels  95.7 us (98%)
  local copies, waits for them, and re-layouts  1.7 us (2%)
    pallas_call x1, Pallas kernels, run_experts(): pl.pallas_call(functools.partial(expert_kernel, n_exp // 2), out_shape=ja...  95.7 us

profile of v4, /device:TPU:1, one launch (start us, length us, event | category | flops | bytes accessed | tf_op | source)
XLA Modules:
  0.0 97.4 jit_solution(14632559143712769286)
XLA Ops:
  0.0 95.7 %experts.1 = bf16[128,1152]{1,0:T(8,128)(2,1)} custom-call(bf16[2,144,1152]{2,1,0:T(8,128)(2,1)} %bitcast.19, bf16[2,144,1152]{2,1,0:T(8,128)(2,1)} %bitcast.20, bf16[2,144,1152]{2,1,0:T(8,128)(2,1)} %bitcast.21, s32[2]{0:T(128)} %levels_ref.1, bf16[128,1152]{1,0:T(8,128)(2,1)} %bitcast.22, bf16[128,1152]{1,0:T(8,128)(2,1)} %bitcast.23, ...), custom_call_target="tpu_custom_call" | custom-call | tf_op jit(solution)/shard_map/experts/pallas_call | solution.py:483
  95.7 1.7 %copy.11 = bf16[2,64,1152]{2,1,0:T(8,128)(2,1)} copy(bf16[2,64,1152]{2,1,0:T(8,128)(2,1)} %bitcast.18) | data formatting | bytes 589824

commit v5 on v4

--- a/solution.py
+++ b/solution.py
@@ -413,19 +413,20 @@
     send_plain(0, 3, 1, o_part[1])
     pass_on(2)
     pass_on(3)
-    compute((1, 2), middle, chunks)
-    send_plain(1, 1, 3, l_part[3])
-    send_plain(2, 2, 2, r_part[2])
     send_added(1, 1, 0, l_part[0])
     send_added(2, 2, 1, r_part[1])
+    compute((1,), middle, chunks)
+    send_plain(1, 1, 3, l_part[3])
     tf_copy[2].wait_recv()
     tf_copy[3].wait_recv()
     compute((3,), middle, chunks)
     send_plain(0, 3, 2, o_part[2])
     send_plain(0, 3, 3, o_part[3])
     finish(0, middle, (0, 1))
+    compute((2,), middle, chunks)
+    send_plain(2, 2, 2, r_part[2])
+    send_added(2, 2, 3, r_part[3])
     send_added(1, 1, 2, l_part[2])
-    send_added(2, 2, 3, r_part[3])
     finish(middle, chunks, (2, 3))
 
     for group in (

time: 97.5 us -> 96.6 us (level)
  no operation moved by 1% of the time
where the time goes in v5:
time: 96.6 us; the launch traced here: 96.5 us
  Pallas kernels  94.8 us (98%)
  local copies, waits for them, and re-layouts  1.7 us (2%)
    pallas_call x1, Pallas kernels, run_experts(): pl.pallas_call(functools.partial(expert_kernel, n_exp // 2), out_shape=ja...  94.8 us

profile of v5, /device:TPU:1, one launch (start us, length us, event | category | flops | bytes accessed | tf_op | source)
XLA Modules:
  0.0 96.5 jit_solution(10374390385907896402)
XLA Ops:
  0.0 94.8 %experts.1 = bf16[128,1152]{1,0:T(8,128)(2,1)} custom-call(bf16[2,144,1152]{2,1,0:T(8,128)(2,1)} %bitcast.19, bf16[2,144,1152]{2,1,0:T(8,128)(2,1)} %bitcast.20, bf16[2,144,1152]{2,1,0:T(8,128)(2,1)} %bitcast.21, s32[2]{0:T(128)} %levels_ref.1, bf16[128,1152]{1,0:T(8,128)(2,1)} %bitcast.22, bf16[128,1152]{1,0:T(8,128)(2,1)} %bitcast.23, ...), custom_call_target="tpu_custom_call" | custom-call | tf_op jit(solution)/shard_map/experts/pallas_call | solution.py:484
  94.8 1.7 %copy.11 = bf16[2,64,1152]{2,1,0:T(8,128)(2,1)} copy(bf16[2,64,1152]{2,1,0:T(8,128)(2,1)} %bitcast.18) | data formatting | bytes 589824
